TPU v7x, 32 devices: a whole 2x2x4 slice. The times are simulated.
32 devices in a mesh: group: 2 (over y), ctx: 4 (over x, core), head: 4 (over z).
Axes of the slice: x: 2, y: 2, z: 4, core: 2. Of those that a mesh axis runs over, the one named last changes fastest.
Arguments:
- activations: bfloat16 [4096, 2304], P(('group', 'ctx', 'head')), parts along dimension 0, may hold values from -6 to 6
- w_query: bfloat16 [2304, 4096], P(None, 'head'), may hold values from -0.125 to 0.125
- w_key: bfloat16 [2304, 4096], P(None, 'head'), may hold values from -0.125 to 0.125
- w_value: bfloat16 [2304, 4096], P(None, 'head'), may hold values from -0.125 to 0.125
- conv_weight: float32 [4, 3, 4096], P(None, None, 'head'), may hold values from -3 to 3
- gate_down: bfloat16 [2304, 128], replicated, may hold values from -0.125 to 0.125
- gate_up: bfloat16 [128, 4096], P(None, 'head'), may hold values from -0.5 to 0.5
- w_beta: bfloat16 [2304, 32], P(None, 'head'), may hold values from -0.125 to 0.125
- decay_rate: float32 [32], P('head'), may hold values from 0 to 1, as said below
- fork_pos: int32 [4], P('group'), parts along dimension 0, may hold values from 0 to 2047, as said below
Outputs:
- attended: bfloat16 [4096, 4096], P(('group', 'ctx'), 'head'), parts along dimension 0
- fork_states: float32 [4, 32, 128, 128], P('group', 'head'), parts along dimension 0
There are 2 independent parts, one for each index of `group`. A program takes and returns all parts, laid end to end along the dimension named above; an argument that names none is the same for every part. Nothing has to cross between parts.
Inputs may be any that keep to these rules, and one draw needn't show every extreme that they name: fork_pos[f] lies in [f * 1024, (f + 1) * 1024); the last one is 2047. `decay_rate`: positive rates.
All inputs are finite; a program needn't handle non-finite values.
Results may differ from a plain program's by a relative error of at most 0.0065.
Values may be sent and summed in bfloat16 or wider, within the bound.
A program may use at most 128 MiB of HBM per device.

v0:
```python
import math

import jax
import jax.numpy as jnp
from jax import lax
from jax.sharding import PartitionSpec as P

BLOCK = 64


EXACT_MATMUL = lax.Precision.HIGHEST


def shifted(value, axis, by):
    size = lax.axis_size(axis)
    pairs = [(i, i + by) for i in range(size) if 0 <= i + by < size]
    return lax.ppermute(value, axis, pairs)


def heads_matmul(left, right):
    return jnp.einsum("hij,hjk->hik", left, right, precision=EXACT_MATMUL)


def to_blocks(values, num_blocks, num_heads):
    return values.reshape(num_blocks, BLOCK, num_heads, -1).transpose(2, 0, 1, 3)


def compose_local(accum, item):
    trans_now, offset_now = item
    return (
        (heads_matmul(trans_now, accum[0]), heads_matmul(trans_now, accum[1]) + offset_now),
        None,
    )


def advance_block(memory_state, item):
    trans_now, offset_now = item
    return (heads_matmul(trans_now, memory_state) + offset_now, memory_state)


def per_device(
    activations,
    w_query,
    w_key,
    w_value,
    conv_weight,
    gate_down,
    gate_up,
    w_beta,
    decay_rate,
    fork_pos,
):
    gathered = lax.all_gather(activations, "head", axis=0, tiled=True)
    seq_len = gathered.shape[0]
    num_heads = w_beta.shape[1]
    head_cols = w_query.shape[1]
    head_dim = head_cols // num_heads
    taps = conv_weight.shape[0]
    projected = jnp.stack(
        [
            jnp.dot(gathered, weights, preferred_element_type=jnp.float32).astype(jnp.bfloat16)
            for weights in (w_query, w_key, w_value)
        ]
    )
    earlier_rows = shifted(projected[:, seq_len - taps + 1 :, :], "ctx", 1)
    extended = jnp.concatenate([earlier_rows, projected], axis=1).astype(jnp.float32)
    mixed = sum(
        (conv_weight[tap][:, None, :] * extended[:, tap : tap + seq_len, :] for tap in range(taps))
    )
    activated = jax.nn.silu(mixed).reshape(3, seq_len, num_heads, head_dim)
    query_vector = (
        activated[0]
        * lax.rsqrt(jnp.sum(jnp.square(activated[0]), axis=-1, keepdims=True) + 1e-06)
        / math.sqrt(head_dim)
    )
    key = activated[1] * lax.rsqrt(
        jnp.sum(jnp.square(activated[1]), axis=-1, keepdims=True) + 1e-06
    )
    value = activated[2]
    latent = jnp.dot(gathered, gate_down, preferred_element_type=jnp.float32).astype(jnp.bfloat16)
    gate_pre = jnp.dot(latent, gate_up, preferred_element_type=jnp.float32).reshape(
        seq_len, num_heads, head_dim
    )
    log_decay = -decay_rate[None, :, None] * jax.nn.softplus(gate_pre)
    beta = jax.nn.sigmoid(jnp.dot(gathered, w_beta, preferred_element_type=jnp.float32))
    num_blocks = seq_len // BLOCK
    query_b = to_blocks(query_vector, num_blocks, num_heads)
    key_b = to_blocks(key, num_blocks, num_heads)
    value_b = to_blocks(value, num_blocks, num_heads)
    decay_b = to_blocks(log_decay, num_blocks, num_heads)
    beta_b = beta.reshape(num_blocks, BLOCK, num_heads).transpose(2, 0, 1)
    cumulative = jnp.cumsum(decay_b, axis=2)
    growth = jnp.exp(cumulative)
    key_up = key_b * growth
    key_down = key_b * jnp.exp(-cumulative)
    query_up = query_b * growth
    pair_keys = jnp.einsum("hnrd,hnsd->hnrs", key_up, key_down, precision=EXACT_MATMUL)
    pair_query = jnp.einsum("hnrd,hnsd->hnrs", query_up, key_down, precision=EXACT_MATMUL)
    places = jnp.arange(BLOCK)
    pair_keys = jnp.where(places[:, None] > places[None, :], pair_keys, 0.0)
    pair_query = jnp.where(places[:, None] >= places[None, :], pair_query, 0.0)
    system = jnp.eye(BLOCK, dtype=jnp.float32) + beta_b[..., None] * pair_keys
    first_part = jax.scipy.linalg.solve_triangular(
        system, beta_b[..., None] * value_b, lower=True, unit_diagonal=True
    )
    second_part = jax.scipy.linalg.solve_triangular(
        system, beta_b[..., None] * key_up, lower=True, unit_diagonal=True
    )
    key_end = key_b * jnp.exp(cumulative[:, :, -1:, :] - cumulative)
    identity_matrix = jnp.eye(head_dim, dtype=jnp.float32)
    transitions = growth[:, :, -1, :, None] * identity_matrix - jnp.einsum(
        "hncd,hnce->hnde", key_end, second_part, precision=EXACT_MATMUL
    )
    offsets = jnp.einsum("hncd,hnce->hnde", key_end, first_part, precision=EXACT_MATMUL)
    trans_seq = transitions.transpose(1, 0, 2, 3)
    offset_seq = offsets.transpose(1, 0, 2, 3)
    eye_heads = jnp.broadcast_to(identity_matrix, (num_heads, head_dim, head_dim))
    zero_state = jnp.zeros((num_heads, head_dim, head_dim), jnp.float32)
    (device_trans, device_offset), unused = lax.scan(
        compose_local, (eye_heads, zero_state), (trans_seq, offset_seq)
    )

    def pass_along(turn, incoming):
        return shifted(heads_matmul(device_trans, incoming) + device_offset, "ctx", 1)

    start_state = lax.fori_loop(0, lax.axis_size("ctx") - 1, pass_along, zero_state)
    final_state, block_starts = lax.scan(advance_block, start_state, (trans_seq, offset_seq))
    block_starts = block_starts.transpose(1, 0, 2, 3)
    updates = first_part - jnp.einsum(
        "hncd,hnde->hnce", second_part, block_starts, precision=EXACT_MATMUL
    )
    outputs = jnp.einsum("hncd,hnde->hnce", query_up, block_starts, precision=EXACT_MATMUL)
    outputs = outputs + jnp.einsum("hnrs,hnse->hnre", pair_query, updates, precision=EXACT_MATMUL)
    attended = outputs.transpose(1, 2, 0, 3).reshape(seq_len, head_cols).astype(jnp.bfloat16)
    local_pos = fork_pos - lax.axis_index("ctx") * seq_len
    owned = (local_pos >= 0) & (local_pos < seq_len)
    clipped = jnp.clip(local_pos, 0, seq_len - 1)
    which_block = clipped // BLOCK
    inner_pos = clipped % BLOCK
    chosen_start = jnp.take(block_starts, which_block, axis=1)
    chosen_key = jnp.take(key_b, which_block, axis=1)
    chosen_cum = jnp.take(cumulative, which_block, axis=1)
    chosen_update = jnp.take(updates, which_block, axis=1)
    cum_at = jnp.take_along_axis(chosen_cum, inner_pos[None, :, None, None], axis=2)
    keep = (places[None, :] <= inner_pos[:, None])[None, :, :, None]
    scaled_key = jnp.where(
        keep, chosen_key * jnp.exp(jnp.where(keep, cum_at - chosen_cum, 0.0)), 0.0
    )
    fork_local = jnp.exp(cum_at[:, :, 0, :])[..., None] * chosen_start
    fork_local = fork_local + jnp.einsum(
        "hfcd,hfce->hfde", scaled_key, chosen_update, precision=EXACT_MATMUL
    )
    fork_local = jnp.where(owned[None, :, None, None], fork_local, 0.0).transpose(1, 0, 2, 3)
    fork_states = lax.psum(fork_local, "ctx")
    return (attended, fork_states)


def solution(mesh):
    return jax.shard_map(
        per_device,
        mesh=mesh,
        in_specs=(
            P(("group", "ctx", "head"), None),
            P(None, "head"),
            P(None, "head"),
            P(None, "head"),
            P(None, None, "head"),
            P(),
            P(None, "head"),
            P(None, "head"),
            P("head"),
            P("group"),
        ),
        out_specs=(P(("group", "ctx"), "head"), P("group", "head", None, None)),
        check_vma=False,
    )
```

profile of v0, /device:TPU:0, one launch (start us, length us, event | category | flops | bytes accessed | tf_op | source)
XLA Modules:
  0.0 634.9 jit_solution(8622109862917172984)
XLA Ops:
  15.5 46.8 %all-gather.2.cloned.1.call-done = bf16[512,2304]{1,0:T(8,128)(2,1)} async-done(((bf16[128,2304]{1,0:T(8,128)(2,1)}), bf16[512,2304]{1,0:T(8,128)(2,1)}) %all-gather.2.cloned.1.call-update) | async-done | bytes 2359312 | tf_op jit(solution)/shard_map/all_gather | solution.py:53
  67.2 5.2 fusion.61
  89.7 3.7 divide_multiply_fusion
  93.4 3.8 multiply_bitcast_fusion.1
  124.8 4.9 broadcast_multiply_fusion
  131.1 5.3 add_bitcast_fusion
  136.4 315.7 %custom-call.7 = f32[8,8,1,64,64]{3,4,2,1,0:T(8,128)S(1)} custom-call(f32[8,8,1,64,64]{4,3,2,1,0:T(8,128)} %add_bitcast_fusion), custom_call_target="InvertDiagBlocksLowerTriangular" | custom-call | tf_op jit(solution)/shard_map/jit(_solve_triangular)/vmap(vmap())/triangular_solve | solution.py:106
  452.1 5.3 fusion.21
  457.4 3.5 fusion.23
  461.0 5.1 fusion.40
  466.1 8.0 %bitcast_subtract_fusion = f32[8,8,128,128]{3,2,0,1:T(8,128)S(1)} fusion(f32[8,8,64,128]{3,2,1,0:T(8,128)S(1)} %fusion.23, f32[128,128]{1,0:T(8,128)S(1)} %fusion.73, f32[8,8,128]{2,0,1:T(8,128)S(1)} %slice_bitcast_fusion.4, f32[8,8,64,128]{3,1,2,0:T(8,128)S(1)} %copy-done.9), kind=kOutput, calls=%fused_computation.32 | convolution fusion | flops 807403520 | bytes 8486912 | tf_op jit(solution)/shard_map/hncd,hnce->hnde/dot_general | solution.py:111
  476.6 6.8 %convolution_bitcast_fusion = f32[8,8,128,128]{3,2,0,1:T(8,128)S(1)} fusion(f32[8,8,64,128]{3,2,1,0:T(8,128)S(1)} %fusion.21, f32[8,8,64,128]{3,1,2,0:T(8,128)S(1)} %copy-done.9), kind=kOutput, calls=%fused_computation.34 | convolution fusion | flops 805306368 | bytes 8388608 | tf_op jit(solution)/shard_map/hncd,hnce->hnde/dot_general | solution.py:114
  486.0 29.3 %while.37 = (s32[]{:T(128)}, f32[8,128,128]{2,1,0:T(8,128)S(1)}, f32[8,128,128]{2,1,0:T(8,128)S(1)}, f32[8,8,128,128]{3,2,1,0:T(8,128)}, f32[8,8,128,128]{3,2,1,0:T(8,128)}, /*index=5*/s32[]{:T(128)}, s32[]{:T(128)}) while((s32[]{:T(128)}, f32[8,128,128]{2,1,0:T(8,128)S(1)}, f32[8,128,128]{2,1,0:T(8,128)S(1)}, ...), condition=%wide.region_4.6_spmd.clone, body=%wide.region_3.5_spmd.clone.sunk | while | flops 402915328 | bytes 5768802 | solution.py:119
  515.3 25.9 %while.35 = (s32[]{:T(128)}, f32[8,128,128]{2,1,0:T(8,128)S(1)}, f32[8,128,128]{2,1,0:T(8,128)S(1)}, f32[8,128,128]{2,1,0:T(8,128)S(1)}, s32[]{:T(128)}) while((s32[]{:T(128)}, f32[8,128,128]{2,1,0:T(8,128)S(1)}, f32[8,128,128]{2,1,0:T(8,128)S(1)}, f32[8,128,128]{2,1,0:T(8,128)S(1)}, s32[]{:T(128)}) %tuple.92), condition=%wide.region_6.8_spmd, body=%wide.region_5.7_spmd.sunk | while | flops 201457664 | bytes 4194405 | solution.py:126
  516.0 3.9 collective-permute-start
  522.0 6.5 %collective-permute-start = (f32[8,128,128]{2,1,0:T(8,128)S(1)}, f32[8,128,128]{2,1,0:T(8,128)S(1)}, u32[]{:S(2)}, u32[]{:S(2)}) collective-permute-start(f32[8,128,128]{2,1,0:T(8,128)S(1)} %convolution_add_fusion.6), channel_id=1, source_target_pairs={{0,4},{4,8},{8,12},{1,5},{5,9},{9,13},{2,6},{6,10},{10,14},{3,7},{... | collective-permute-start | bytes 1572872 | tf_op jit(solution)/shard_map/while/body/eval_jaxpr/ppermute | solution.py:17
  530.7 9.0 %collective-permute-start = (f32[8,128,128]{2,1,0:T(8,128)S(1)}, f32[8,128,128]{2,1,0:T(8,128)S(1)}, u32[]{:S(2)}, u32[]{:S(2)}) collective-permute-start(f32[8,128,128]{2,1,0:T(8,128)S(1)} %convolution_add_fusion.6), channel_id=1, source_target_pairs={{0,4},{4,8},{8,12},{1,5},{5,9},{9,13},{2,6},{6,10},{10,14},{3,7},{... | collective-permute-start | bytes 1572872 | tf_op jit(solution)/shard_map/while/body/eval_jaxpr/ppermute | solution.py:17
  541.2 22.3 %while.36 = (s32[]{:T(128)}, f32[8,128,128]{2,1,0:T(8,128)S(1)}, f32[8,8,128,128]{3,2,0,1:T(8,128)}, f32[8,8,128,128]{3,2,1,0:T(8,128)}, f32[8,8,128,128]{3,2,1,0:T(8,128)}, /*index=5*/s32[]{:T(128)}) while((s32[]{:T(128)}, f32[8,128,128]{2,1,0:T(8,128)S(1)}, f32[8,8,128,128]{3,2,0,1:T(8,128)}, f32[8,8,128,128]{3,2,1,0:T(8,128)}, ...), condition=%wide.region_8.10_spmd, body=%wide.region_7.9_spmd.sunk | while | flops 201457664 | bytes 4195409 | solution.py:127
  563.5 7.3 %convolution_subtract_fusion = f32[8,8,64,128]{3,2,1,0:T(8,128)S(1)} fusion(f32[8,8,64,128]{3,2,1,0:T(8,128)} %copy-done.3, f32[8,8,64,128]{3,2,1,0:T(8,128)} %copy-done.4, f32[8,8,128,128]{3,2,0,1:T(8,128)} %get-tuple-element.84), kind=kOutput, calls=%fused_computation.78 | convolution fusion | flops 805830656 | bytes 10485760 | tf_op jit(solution)/shard_map/hncd,hnde->hnce/dot_general | solution.py:129
  571.7 3.9 gather_fusion
  577.6 4.6 fusion.58
  582.3 4.1 fusion.31
  586.4 4.2 fusion.54
  592.5 32.9 %all-reduce.2.cloned.1.call-done = f32[2,8,128,128]{3,2,0,1:T(8,128)} async-done(((f32[2,8,128,128]{3,2,0,1:T(8,128)}), f32[2,8,128,128]{3,2,0,1:T(8,128)}) %all-reduce.2.cloned.1.call-update) | async-done | bytes 1048592 | tf_op jit(solution)/shard_map/psum | solution.py:154
  (207 shorter events, 128.4 us)
Async XLA Ops:
  7.2 55.1 %copy-start = (bf16[2304,128]{1,0:T(8,128)(2,1)S(1)}, bf16[2304,128]{1,0:T(8,128)(2,1)}, u32[]{:S(2)}) copy-start(bf16[2304,128]{1,0:T(8,128)(2,1)} %param.25) | copy-start | bytes 1769476
  7.2 55.1 %all-gather.2.cloned.1.call-start = ((), (), s32[]{:S(2)}) async-start(), calls=%async_computation | async-start | bytes 2949120 | tf_op jit(solution)/shard_map/all_gather | solution.py:53
  7.9 617.5 %all-reduce.2.cloned.1.call-start = ((), (), s32[]{:S(2)}) async-start(), calls=%async_computation.1 | async-start | bytes 2097152 | tf_op jit(solution)/shard_map/psum | solution.py:154
  11.2 73.1 %copy-start.26 = (s32[1024]{0:T(1024)}, s32[1024]{0:T(1024)S(1)}, u32[]{:S(2)}) copy-start(s32[1024]{0:T(1024)S(1)} %pad_clamp_fusion) | copy-start | bytes 12292
  65.5 6.9 %slice-start = ((s8[4718592]{0:T(1024)(128)(4,1)}), s8[4194304]{0:T(1024)(128)(4,1)S(1)}, s32[]{:S(2)}) async-start(s8[4718592]{0:T(1024)(128)(4,1)} %bitcast.186), calls=%async_computation.2 | async-start | bytes 8388608
  67.2 5.2 slice-start.1
  67.2 7.9 %slice-start.2 = ((s8[4718592]{0:T(1024)(128)(4,1)}), s8[4194304]{0:T(1024)(128)(4,1)S(1)}, s32[]{:S(2)}) async-start(s8[4718592]{0:T(1024)(128)(4,1)} %bitcast.188), calls=%async_computation.4 | async-start | bytes 8388608
  72.5 5.3 copy-start.17
  77.8 9.5 %collective-permute-start.1 = (bf16[3,3,1024]{2,1,0:T(4,128)(2,1)S(1)}, bf16[3,3,1024]{2,1,0:T(4,128)(2,1)S(1)}, u32[]{:S(2)}, u32[]{:S(2)}) collective-permute-start(bf16[3,3,1024]{2,1,0:T(4,128)(2,1)S(1)} %pad_maximum_fusion), channel_id=1, source_target_pairs={{0,4},{4,8},{8,12},{1,5},{5,9},{9,13},{2,6},{6,10},{10,14},{3,7},{... | collective-permute-start | bytes 55304 | tf_op jit(solution)/shard_map/ppermute | solution.py:17
  124.8 6.4 %copy-start.20 = (f32[64,64]{1,0:T(8,128)S(1)}, f32[64,64]{1,0:T(8,128)}, u32[]{:S(2)}) copy-start(f32[64,64]{1,0:T(8,128)} %get-tuple-element.212) | copy-start | bytes 49156
  124.8 6.4 %copy-start.21 = (f32[64,64]{1,0:T(8,128)S(1)}, f32[64,64]{1,0:T(8,128)}, u32[]{:S(2)}) copy-start(f32[64,64]{1,0:T(8,128)} %get-tuple-element.213) | copy-start | bytes 49156
  124.8 6.4 %copy-start.24 = (pred[64,64]{1,0:T(8,128)(4,1)S(1)}, pred[64,64]{1,0:T(8,128)(4,1)}, u32[]{:S(2)}) copy-start(pred[64,64]{1,0:T(8,128)(4,1)} %get-tuple-element.210) | copy-start | bytes 12292
  124.8 6.4 %copy-start.25 = (pred[64,64]{1,0:T(8,128)(4,1)S(1)}, pred[64,64]{1,0:T(8,128)(4,1)}, u32[]{:S(2)}) copy-start(pred[64,64]{1,0:T(8,128)(4,1)} %get-tuple-element.211) | copy-start | bytes 12292
  452.1 5.3 copy-start.13
  457.4 19.2 %copy-start.3 = (f32[8,8,64,128]{3,2,1,0:T(8,128)}, f32[8,8,64,128]{3,2,1,0:T(8,128)S(1)}, u32[]{:S(2)}) copy-start(f32[8,8,64,128]{3,2,1,0:T(8,128)S(1)} %fusion.21) | copy-start | bytes 6291460
  460.9 5.1 copy-start.4
  461.0 5.1 copy-start.9
  516.0 5.3 collective-permute-start
  522.0 8.0 %collective-permute-start = (f32[8,128,128]{2,1,0:T(8,128)S(1)}, f32[8,128,128]{2,1,0:T(8,128)S(1)}, u32[]{:S(2)}, u32[]{:S(2)}) collective-permute-start(f32[8,128,128]{2,1,0:T(8,128)S(1)} %convolution_add_fusion.6), channel_id=1, source_target_pairs={{0,4},{4,8},{8,12},{1,5},{5,9},{9,13},{2,6},{6,10},{10,14},{3,7},{... | collective-permute-start | bytes 1572872 | tf_op jit(solution)/shard_map/while/body/eval_jaxpr/ppermute | solution.py:17
  530.7 10.5 %collective-permute-start = (f32[8,128,128]{2,1,0:T(8,128)S(1)}, f32[8,128,128]{2,1,0:T(8,128)S(1)}, u32[]{:S(2)}, u32[]{:S(2)}) collective-permute-start(f32[8,128,128]{2,1,0:T(8,128)S(1)} %convolution_add_fusion.6), channel_id=1, source_target_pairs={{0,4},{4,8},{8,12},{1,5},{5,9},{9,13},{2,6},{6,10},{10,14},{3,7},{... | collective-permute-start | bytes 1572872 | tf_op jit(solution)/shard_map/while/body/eval_jaxpr/ppermute | solution.py:17
  570.8 4.8 copy-start.16
  570.8 4.8 copy-start.27
  577.6 4.7 copy-start.23
  591.3 36.4 %copy-start.1 = (bf16[2304,128]{1,0:T(8,128)(2,1)S(1)}, bf16[2304,128]{1,0:T(8,128)(2,1)}, u32[]{:S(2)}) copy-start(bf16[2304,128]{1,0:T(8,128)(2,1)} %param.25) | copy-start | bytes 1769476
  (18 other events, 44.8 us)
Sparse Core Ops, SparseCore 0:
  9.6 52.6 all-gather.1
  582.4 42.9 all-reduce.1
where the time goes:
time: 642 us; the launch traced here: 635 us
  other arithmetic  347 us (54%)
  matrix products  114 us (18%)
  waiting for transfers between devices  84.8 us (13%)
  local copies, waits for them, and re-layouts  52.1 us (8%)
  starting transfers between devices  21.3 us (3%)
  between operations  15.1 us (2%)
    another operation x3, other arithmetic, per_device(): jax.scipy.linalg.solve_triangular(system, beta_b[..., None] * key_up, low...  316 us
    all_gather x1, waiting for transfers between devices, per_device(): gathered = lax.all_gather(activations, 'head', axis=0, tiled=True)  46.8 us
    dot_general x27, matrix products, heads_matmul(): return jnp.einsum('hij,hjk->hik', left, right, precision=EXACT_MATMUL)  45 us
    psum x1, waiting for transfers between devices, per_device(): fork_states = lax.psum(fork_local, 'ctx')  32.9 us
    unnamed x85, local copies, waits for them, and re-layouts  25.2 us
    ppermute x4, starting transfers between devices, shifted(): return lax.ppermute(value, axis, pairs)  21.2 us
  transfers between devices with their start and end apart: 6, of which 5 were waited for; matrix products, arithmetic and copies ran while one was open for 4% of the time, Pallas kernels for 0%

commit v1 on v0

v1 whole, which is shorter than its diff:
```python
import functools
import math

import jax
import jax.numpy as jnp
from jax import lax
from jax.experimental import pallas as pl
from jax.experimental.pallas import tpu as pltpu
from jax.sharding import PartitionSpec as P

CHUNK = 128
F32 = jnp.float32
BF16 = jnp.bfloat16
NT = (((1,), (1,)), ((), ()))
TN = (((0,), (0,)), ((), ()))


def dot(left, right, dims=None):
    left, right = left.astype(BF16), right.astype(BF16)
    if dims is None:
        return jnp.dot(left, right, preferred_element_type=F32)
    return lax.dot_general(left, right, dims, preferred_element_type=F32)


def softplus(value):
    return jnp.maximum(value, 0.0) + jnp.log1p(jnp.exp(-jnp.abs(value)))


def level_masks():
    row = lax.broadcasted_iota(jnp.int32, (CHUNK, CHUNK), 0)
    col = lax.broadcasted_iota(jnp.int32, (CHUNK, CHUNK), 1)
    masks = {}
    size = 1
    while size < CHUNK:
        same = (row // (2 * size)) == (col // (2 * size))
        masks[size] = same & ((row & size) != 0) & ((col & size) == 0)
        size *= 2
    return row, col, masks


def level_reference(cum, size):
    if size >= 8:
        parts = cum.reshape(CHUNK // (2 * size), 2 * size, cum.shape[1])
        ref = parts[:, size - 1 : size, :]
        return jnp.broadcast_to(ref, parts.shape).reshape(cum.shape)
    parts = cum.reshape(CHUNK // 8, 8, cum.shape[1])
    place = lax.broadcasted_iota(jnp.int32, parts.shape, 1)
    ref = jnp.broadcast_to(parts[:, size - 1 : size, :], parts.shape)
    for start in range(2 * size, 8, 2 * size):
        ref = jnp.where(place >= start, parts[:, start + size - 1 : start + size, :], ref)
    return ref.reshape(cum.shape)


def local_kernel(
    q_ref, k_ref, v_ref, halo_ref, conv_ref, latent_ref, up_ref, beta_ref, rate_ref, pos_ref,
    w_ref, u_ref, qk_ref, qup_ref, kend_ref, dec_ref, kf_ref, df_ref, dev_ref, ext_ref,
):
    head = pl.program_id(0)
    seq_len, dim = q_ref.shape
    acts = []
    for j, src in enumerate((q_ref, k_ref, v_ref)):
        ext_ref[j, 0:8, :] = halo_ref[j].astype(F32)
        ext_ref[j, 8:, :] = src[...].astype(F32)
        taps = conv_ref.shape[0]
        mixed = sum(
            conv_ref[tap, j : j + 1, :] * ext_ref[j, 9 - taps + tap : 9 - taps + tap + seq_len, :]
            for tap in range(taps)
        )
        acts.append(mixed / (1.0 + jnp.exp(-mixed)))
    query = acts[0] * (
        lax.rsqrt(jnp.sum(acts[0] * acts[0], axis=-1, keepdims=True) + 1e-06) / math.sqrt(dim)
    )
    key = acts[1] * lax.rsqrt(jnp.sum(acts[1] * acts[1], axis=-1, keepdims=True) + 1e-06)
    value = acts[2]
    gate = jnp.dot(latent_ref[...], up_ref[...], preferred_element_type=F32)
    decay = -rate_ref[head] * softplus(gate)
    lane = lax.broadcasted_iota(jnp.int32, beta_ref.shape, 1)
    beta = jnp.sum(jnp.where(lane == head, beta_ref[...], 0.0), axis=1, keepdims=True)
    beta = 1.0 / (1.0 + jnp.exp(-beta))
    row, col, masks = level_masks()
    tril = (row >= col).astype(BF16)
    eye = (row == col).astype(F32)
    pos = pos_ref[0]
    stacked = jnp.concatenate([eye, jnp.zeros((dim, dim), F32)], axis=0)
    kf_ref[0] = jnp.zeros((CHUNK, dim), BF16)
    df_ref[0] = jnp.zeros((8, dim), F32)
    for c in range(seq_len // CHUNK):
        rows = slice(c * CHUNK, (c + 1) * CHUNK)
        g, qc, kc, vc, bc = decay[rows], query[rows], key[rows], value[rows], beta[rows]
        high = g.astype(BF16)
        low = (g - high.astype(F32)).astype(BF16)
        both = jnp.dot(tril, jnp.concatenate([high, low], axis=1), preferred_element_type=F32)
        cum = both[:, :dim] + both[:, dim:]
        pair_k = jnp.zeros((CHUNK, CHUNK), F32)
        pair_q = jnp.where(
            row == col, jnp.sum(qc.astype(BF16).astype(F32) * kc.astype(BF16).astype(F32), axis=1, keepdims=True), 0.0
        )
        for size, mask in masks.items():
            scale = jnp.exp(-jnp.abs(cum - level_reference(cum, size)))
            ks = (kc * scale).astype(BF16)
            qs = (qc * scale).astype(BF16)
            pairs = dot(jnp.concatenate([ks, qs], axis=0), ks, NT)
            pair_k = jnp.where(mask, pairs[:CHUNK], pair_k)
            pair_q = jnp.where(mask, pairs[CHUNK:], pair_q)
        system = bc * pair_k
        inverse = eye - jnp.where(masks[1], system, 0.0)
        for size, mask in masks.items():
            if size > 1:
                inverse = inverse - dot(dot(inverse, jnp.where(mask, system, 0.0)), inverse)
        grown = jnp.exp(cum)
        solved = dot(inverse, jnp.concatenate([bc * vc, bc * (kc * grown)], axis=1))
        u, w = solved[:, :dim], solved[:, dim:].astype(BF16)
        last = cum[CHUNK - 1 : CHUNK, :]
        kend = (kc * jnp.exp(last - cum)).astype(BF16)
        whole = jnp.exp(last)
        u_ref[rows, :] = u
        w_ref[rows, :] = w
        qk_ref[rows, :] = pair_q.astype(BF16)
        qup_ref[rows, :] = (qc * grown).astype(BF16)
        kend_ref[rows, :] = kend
        dec_ref[0, c : c + 1, :] = whole
        change = jnp.concatenate([jnp.zeros((CHUNK, dim), F32), u], axis=1) - dot(w, stacked, NT)
        stacked = stacked * whole + dot(change, kend, TN)

        @pl.when((pos >= c * CHUNK) & (pos < (c + 1) * CHUNK))
        def _():
            inner = pos - c * CHUNK
            at = jnp.sum(jnp.where(row[:, :1] == inner, cum, 0.0), axis=0, keepdims=True)
            keep = row[:, :1] <= inner
            kf_ref[0] = jnp.where(keep, kc * jnp.exp(jnp.minimum(at - cum, 0.0)), 0.0).astype(BF16)
            df_ref[0] = jnp.broadcast_to(jnp.exp(at), (8, dim))

    dev_ref[0] = stacked


def read_kernel(
    start_ref, w_ref, u_ref, qk_ref, qup_ref, kend_ref, dec_ref, kf_ref, df_ref, pos_ref,
    out_ref, fork_ref,
):
    seq_len, dim = w_ref.shape
    state = start_ref[0]
    pos = pos_ref[0]
    fork_ref[0] = jnp.zeros((dim, dim), BF16)
    for c in range(seq_len // CHUNK):
        rows = slice(c * CHUNK, (c + 1) * CHUNK)
        both = dot(jnp.concatenate([w_ref[rows, :], qup_ref[rows, :]], axis=0), state, NT)
        change = (u_ref[rows, :] - both[:CHUNK]).astype(BF16)
        out_ref[rows, :] = (both[CHUNK:] + dot(qk_ref[rows, :], change)).astype(BF16)

        @pl.when((pos >= c * CHUNK) & (pos < (c + 1) * CHUNK))
        def _():
            saved = state * df_ref[0, 0:1, :] + dot(change, kf_ref[0], TN)
            fork_ref[0] = saved.T.astype(BF16)

        state = state * dec_ref[0, c : c + 1, :] + dot(change, kend_ref[rows, :], TN)


def shifted(value, axis, by):
    size = lax.axis_size(axis)
    pairs = [(i, i + by) for i in range(size) if 0 <= i + by < size]
    return lax.ppermute(value, axis, pairs)


def per_device(
    activations, w_query, w_key, w_value, conv_weight, gate_down, gate_up, w_beta, decay_rate, fork_pos
):
    gathered = lax.all_gather(activations, "head", axis=0, tiled=True)
    seq_len = gathered.shape[0]
    num_heads = w_beta.shape[1]
    head_cols = w_query.shape[1]
    dim = head_cols // num_heads
    num_ctx = lax.axis_size("ctx")
    num_forks = fork_pos.shape[0]
    per_fork = num_ctx // num_forks
    projected = [
        jnp.dot(gathered, weights, preferred_element_type=F32).astype(BF16)
        for weights in (w_query, w_key, w_value)
    ]
    halo = shifted(jnp.stack([p[seq_len - 8 :] for p in projected]), "ctx", 1)
    latent = jnp.dot(gathered, gate_down, preferred_element_type=F32).astype(BF16)
    beta_pre = jnp.dot(gathered, w_beta, preferred_element_type=F32)
    ctx = lax.axis_index("ctx")
    pos = lax.dynamic_slice(fork_pos, (ctx // per_fork,), (1,)) - ctx * seq_len
    chunks = seq_len // CHUNK

    column = pl.BlockSpec((seq_len, dim), lambda h: (0, h))
    per_head = lambda *shape: pl.BlockSpec((1,) + shape, lambda h: (h,) + (0,) * len(shape))
    smem = pl.BlockSpec(memory_space=pltpu.SMEM)
    whole = lambda *shape: pl.BlockSpec(shape, lambda h: (0,) * len(shape))
    cols = lambda dtype: jax.ShapeDtypeStruct((seq_len, head_cols), dtype)
    heads = lambda dtype, *shape: jax.ShapeDtypeStruct((num_heads,) + shape, dtype)
    w, u, qk, qup, kend, dec, kf, df, dev = pl.pallas_call(
        local_kernel,
        grid=(num_heads,),
        in_specs=[
            column, column, column,
            pl.BlockSpec((3, 8, dim), lambda h: (0, 0, h)),
            pl.BlockSpec((conv_weight.shape[0], 3, dim), lambda h: (0, 0, h)),
            whole(seq_len, latent.shape[1]),
            pl.BlockSpec((latent.shape[1], dim), lambda h: (0, h)),
            whole(seq_len, num_heads), smem, smem,
        ],
        out_specs=[
            column, column, column, column, column,
            per_head(chunks, dim), per_head(CHUNK, dim), per_head(8, dim), per_head(2 * dim, dim),
        ],
        out_shape=[
            cols(BF16), cols(F32), cols(BF16), cols(BF16), cols(BF16),
            heads(F32, chunks, dim), heads(BF16, CHUNK, dim), heads(F32, 8, dim), heads(F32, 2 * dim, dim),
        ],
        scratch_shapes=[pltpu.VMEM((3, seq_len + 8, dim), F32)],
        name="local",
    )(*projected, halo, conv_weight, latent, gate_up, beta_pre, decay_rate, pos)

    trans, offset = dev[:, :dim], dev[:, dim:]
    start = jnp.zeros((num_heads, dim, dim), F32)
    for turn in range(num_ctx - 1):
        end = offset if turn == 0 else offset + jnp.einsum(
            "hij,hjk->hik", start, trans, precision=lax.Precision.HIGH
        )
        start = shifted(end.astype(BF16), "ctx", 1).astype(F32)

    attended, fork_local = pl.pallas_call(
        read_kernel,
        grid=(num_heads,),
        in_specs=[
            per_head(dim, dim), column, column, column, column, column,
            per_head(chunks, dim), per_head(CHUNK, dim), per_head(8, dim), smem,
        ],
        out_specs=[column, per_head(dim, dim)],
        out_shape=[cols(BF16), heads(BF16, dim, dim)],
        name="read",
    )(start, w, u, qk, qup, kend, dec, kf, df, pos)
    everyone = lax.all_gather(fork_local, "ctx", axis=0)
    fork_states = everyone.reshape((num_forks, per_fork) + fork_local.shape).astype(F32).sum(axis=1)
    return attended, fork_states


def solution(mesh):
    return jax.shard_map(
        per_device,
        mesh=mesh,
        in_specs=(
            P(("group", "ctx", "head"), None),
            P(None, "head"),
            P(None, "head"),
            P(None, "head"),
            P(None, None, "head"),
            P(),
            P(None, "head"),
            P(None, "head"),
            P("head"),
            P("group"),
        ),
        out_specs=(P(("group", "ctx"), "head"), P("group", "head", None, None)),
        check_vma=False,
    )
```

time: 642 us -> 232 us (0.36)
  other arithmetic: 347 us -> 3.31 us
  Pallas kernels: 0 us -> 97.6 us
  matrix products: 114 us -> 19.7 us
  local copies, waits for them, and re-layouts: 52.1 us -> 4.44 us
  waiting for transfers between devices: 84.8 us -> 74.7 us
    another operation x5 -> x1, other arithmetic: 318 us -> 0.01 us  [per_device(): halo = shifted(jnp.stack([p[seq_len - 8:] for p in projected]), 'ctx', 1)]
    pallas_call x0 -> x2, Pallas kernels: none -> 97.6 us  [the longest x1 80.1 us: per_device(): pl.pallas_call(local_kernel, grid=(num_heads,), in_specs=[column, column,...]
    dot_general x40 -> x7, matrix products: 105 us -> 19.7 us  [the longest x3 13.8 us: per_device(): jnp.dot(gathered, weights, preferred_element_type=F32).astype(BF16)]
    psum x1 -> x0, waiting for transfers between devices: 32.9 us -> none  [per_device(): fork_states = lax.psum(fork_local, 'ctx')]
    unnamed x85 -> x19, local copies, waits for them, and re-layouts: 25.2 us -> 2.11 us
    all_gather x0 -> x1, waiting for transfers between devices: none -> 19.7 us  [per_device(): everyone = lax.all_gather(fork_local, 'ctx', axis=0)]
    mul x4 -> x0, other arithmetic: 11.5 us -> none  [the longest x1 4.94 us: per_device(): beta_b[..., None] * key_up]
    gather x6 -> x0, local copies, waits for them, and re-layouts: 11.5 us -> none  [the longest x1 3.89 us: per_device(): chosen_start = jnp.take(block_starts, which_block, axis=1)]
  transfers between devices with their start and end apart: 6 -> 6, of which waited for: 5 -> 5; matrix products, arithmetic and copies ran while one was open for 4% -> 2% of each run, Pallas kernels for 0% -> 0%
where the time goes in v1:
time: 232 us; the launch traced here: 231 us
  Pallas kernels  97.6 us (42%)
  waiting for transfers between devices  74.7 us (32%)
  matrix products  19.7 us (8%)
  starting transfers between devices  16.4 us (7%)
  between operations  14.9 us (6%)
  local copies, waits for them, and re-layouts  4.44 us (2%)
  other arithmetic  3.31 us (1%)
    pallas_call x1, Pallas kernels, per_device(): pl.pallas_call(local_kernel, grid=(num_heads,), in_specs=[column, column,...  80.1 us
    all_gather x1, waiting for transfers between devices, per_device(): gathered = lax.all_gather(activations, 'head', axis=0, tiled=True)  51 us
    all_gather x1, waiting for transfers between devices, per_device(): everyone = lax.all_gather(fork_local, 'ctx', axis=0)  19.7 us
    pallas_call x1, Pallas kernels, per_device(): pl.pallas_call(read_kernel, grid=(num_heads,), in_specs=[per_head(dim, di...  17.5 us
    ppermute x4, starting transfers between devices, shifted(): return lax.ppermute(value, axis, pairs)  16.3 us
    dot_general x3, matrix products, per_device(): jnp.dot(gathered, weights, preferred_element_type=F32).astype(BF16)  13.8 us
  transfers between devices with their start and end apart: 6, of which 5 were waited for; matrix products, arithmetic and copies ran while one was open for 2% of the time, Pallas kernels for 0%

profile of v1, /device:TPU:0, one launch (start us, length us, event | category | flops | bytes accessed | tf_op | source)
XLA Modules:
  0.0 231.1 jit_solution(17950411269294396346)
XLA Ops:
  7.2 0.7 all-gather.4.cloned.1.call-update
  8.0 1.4 copy.14.conv_ref
  9.4 1.2 dynamic_slice.3
  11.3 51.0 %all-gather.4.cloned.1.call-done = bf16[512,2304]{1,0:T(8,128)(2,1)} async-done(((bf16[128,2304]{1,0:T(8,128)(2,1)}), bf16[512,2304]{1,0:T(8,128)(2,1)}) %all-gather.4.cloned.1.call-update) | async-done | bytes 2359312 | tf_op jit(solution)/shard_map/all_gather | solution.py:167
  62.3 5.8 %convolution_convert_fusion.2.q_ref = bf16[512,1024]{1,0:T(8,128)(2,1)S(1)} fusion(bf16[512,2304]{1,0:T(8,128)(2,1)} %all-gather.4.cloned.1.call-done, bf16[2304,1024]{1,0:T(8,128)(2,1)} %param.11), kind=kOutput, calls=%fused_computation.3 | convolution fusion | flops 2416443392 | bytes 8126464 | tf_op jit(solution)/shard_map/dot_general | solution.py:176
  68.1 5.4 %convolution_convert_fusion.v_ref = bf16[512,1024]{1,0:T(8,128)(2,1)S(1)} fusion(bf16[512,2304]{1,0:T(8,128)(2,1)S(1)} %copy-done.5, bf16[2304,1024]{1,0:T(8,128)(2,1)} %param.13), kind=kOutput, calls=%fused_computation.1 | convolution fusion | flops 2416443392 | bytes 8126464 | tf_op jit(solution)/shard_map/dot_general | solution.py:176
  73.6 2.6 %convolution_convert_fusion.1.k_ref = bf16[512,1024]{1,0:T(8,128)(2,1)S(1)} fusion(bf16[512,2304]{1,0:T(8,128)(2,1)S(1)} %copy-done.5, bf16[2304,1024]{1,0:T(8,128)(2,1)S(1)} %bitcast.23), kind=kOutput, calls=%fused_computation.2 | convolution fusion | flops 2416443392 | bytes 8126464 | tf_op jit(solution)/shard_map/dot_general | solution.py:176
  76.3 1.6 collective-permute-start
  77.9 1.5 convolution_convert_fusion.3.latent_ref
  79.3 1.5 fusion.4.beta_ref
  81.4 80.1 %local.1 = (bf16[512,1024]{1,0:T(8,128)(2,1)}, f32[512,1024]{1,0:T(8,128)}, bf16[512,1024]{1,0:T(8,128)(2,1)}, bf16[512,1024]{1,0:T(8,128)(2,1)}, bf16[512,1024]...) custom-call(bf16[512,1024]{1,0:T(8,128)(2,1)} %copy-done.1, ...), custom_call_target="tpu_custom_call" | custom-call | tf_op jit(solution)/shard_map/local/pallas_call | solution.py:192
  161.5 1.1 slice.33
  162.6 3.5 %collective-permute-start.1 = (bf16[8,128,128]{2,1,0:T(8,128)(2,1)S(1)}, bf16[8,128,128]{2,1,0:T(8,128)(2,1)S(1)}, u32[]{:S(2)}, u32[]{:S(2)}) collective-permute-start(bf16[8,128,128]{2,1,0:T(8,128)(2,1)S(1)} %slice.33), channel_id=1, source_target_pairs={{0,4},{4,8},{8,12},{1,5},{5,9},{9,13},{2,6},{6,10},{10,14},{3,7},{... | collective-permute-start | bytes 786440 | tf_op jit(solution)/shard_map/ppermute | solution.py:161
  166.2 1.1 collective-permute-done.1
  167.3 1.5 fusion
  168.8 4.6 %collective-permute-start.2 = (bf16[8,128,128]{2,1,0:T(8,128)(2,1)S(1)}, bf16[8,128,128]{2,1,0:T(8,128)(2,1)S(1)}, u32[]{:S(2)}, u32[]{:S(2)}) collective-permute-start(bf16[8,128,128]{2,1,0:T(8,128)(2,1)S(1)} %fusion), channel_id=1, source_target_pairs={{0,4},{4,8},{8,12},{1,5},{5,9},{9,13},{2,6},{6,10},{10,14},{3,7},{... | collective-permute-start | bytes 786440 | tf_op jit(solution)/shard_map/ppermute | solution.py:161
  173.5 1.1 collective-permute-done.2
  174.6 1.5 fusion.1
  176.1 6.6 %collective-permute-start.3 = (bf16[8,128,128]{2,1,0:T(8,128)(2,1)S(1)}, bf16[8,128,128]{2,1,0:T(8,128)(2,1)S(1)}, u32[]{:S(2)}, u32[]{:S(2)}) collective-permute-start(bf16[8,128,128]{2,1,0:T(8,128)(2,1)S(1)} %fusion.1), channel_id=1, source_target_pairs={{0,4},{4,8},{8,12},{1,5},{5,9},{9,13},{2,6},{6,10},{10,14},{3,7},{... | collective-permute-start | bytes 786440 | tf_op jit(solution)/shard_map/ppermute | solution.py:161
  182.7 1.1 collective-permute-done.3
  183.8 0.8 convert_element_type.39.start_ref
  184.6 17.5 %read.1 = (bf16[512,1024]{1,0:T(8,128)(2,1)}, bf16[8,128,128]{2,1,0:T(8,128)(2,1)}) custom-call(f32[8,128,128]{2,1,0:T(8,128)} %convert_element_type.39.start_ref, bf16[512,1024]{1,0:T(8,128)(2,1)} %get-tuple-element.14.w_ref, f32[512,1024]{1,0:T(8,128)} %get-tuple-element.15.u_ref, bf16[512,1024]{1,0:T(8,128)(2,1)} %get-tuple-element.16.qk_ref, ...), custom_call_target="tpu_custom_call" | custom-call | tf_op jit(solution)/shard_map/read/pallas_call | solution.py:223
  202.1 19.7 %all-gather.6.cloned.1.call-done = bf16[32,128,128]{2,1,0:T(8,128)(2,1)} async-done(((bf16[8,128,128]{2,1,0:T(8,128)(2,1)}), bf16[32,128,128]{2,1,0:T(8,128)(2,1)}) %all-gather.6.cloned.1.call-update) | async-done | bytes 1048592 | tf_op jit(solution)/shard_map/all_gather | solution.py:234
  221.8 2.5 %convert_reduce_fusion = f32[2,8,128,128]{3,2,1,0:T(8,128)} fusion(bf16[2,2,8,128,128]{4,3,2,1,0:T(8,128)(2,1)} %bitcast.21), kind=kLoop, calls=%fused_computation | loop fusion | flops 786432 | bytes 2097152 | tf_op jit(solution)/shard_map/reduce_sum | solution.py:235
  (26 shorter events, 0.8 us)
Async XLA Ops:
  7.2 70.7 %copy-start = (bf16[2304,128]{1,0:T(8,128)(2,1)S(1)}, bf16[2304,128]{1,0:T(8,128)(2,1)}, u32[]{:S(2)}) copy-start(bf16[2304,128]{1,0:T(8,128)(2,1)} %param.15) | copy-start | bytes 1769476
  7.2 55.1 %all-gather.4.cloned.1.call-start = ((), (), s32[]{:S(2)}) async-start(), calls=%async_computation | async-start | bytes 2949120 | tf_op jit(solution)/shard_map/all_gather | solution.py:167
  7.9 213.9 %all-gather.6.cloned.1.call-start = ((), (), s32[]{:S(2)}) async-start(), calls=%async_computation.1 | async-start | bytes 1310720 | tf_op jit(solution)/shard_map/all_gather | solution.py:234
  62.3 5.8 %copy-start.5 = (bf16[512,2304]{1,0:T(8,128)(2,1)S(1)}, bf16[512,2304]{1,0:T(8,128)(2,1)}, u32[]{:S(2)}) copy-start(bf16[512,2304]{1,0:T(8,128)(2,1)} %all-gather.4.cloned.1.call-done) | copy-start | bytes 7077892
  62.3 11.3 %slice-start = ((s8[4718592]{0:T(1024)(128)(4,1)}), s8[4194304]{0:T(1024)(128)(4,1)S(1)}, s32[]{:S(2)}) async-start(s8[4718592]{0:T(1024)(128)(4,1)} %bitcast.22), calls=%async_computation.2 | async-start | bytes 8388608
  68.1 5.5 %copy-start.1 = (bf16[512,1024]{1,0:T(8,128)(2,1)}, bf16[512,1024]{1,0:T(8,128)(2,1)S(1)}, u32[]{:S(2)}) copy-start(bf16[512,1024]{1,0:T(8,128)(2,1)S(1)} %convolution_convert_fusion.2.q_ref) | copy-start | bytes 3145732
  68.1 5.5 %slice-start.1 = ((s8[4718592]{0:T(1024)(128)(4,1)}), s8[524288]{0:T(1024)(128)(4,1)S(1)}, s32[]{:S(2)}) async-start(s8[4718592]{0:T(1024)(128)(4,1)} %bitcast.22), calls=%async_computation.3 | async-start | bytes 1048576
  73.6 2.6 %copy-start.2 = (bf16[512,1024]{1,0:T(8,128)(2,1)}, bf16[512,1024]{1,0:T(8,128)(2,1)S(1)}, u32[]{:S(2)}) copy-start(bf16[512,1024]{1,0:T(8,128)(2,1)S(1)} %convolution_convert_fusion.v_ref) | copy-start | bytes 3145732
  76.2 4.6 %copy-start.3 = (bf16[512,1024]{1,0:T(8,128)(2,1)}, bf16[512,1024]{1,0:T(8,128)(2,1)S(1)}, u32[]{:S(2)}) copy-start(bf16[512,1024]{1,0:T(8,128)(2,1)S(1)} %convolution_convert_fusion.1.k_ref) | copy-start | bytes 3145732
  76.2 3.1 %copy-start.6 = (bf16[2304,8]{0,1:T(8,128)(2,1)S(1)}, bf16[2304,8]{0,1:T(8,128)(2,1)}, u32[]{:S(2)}) copy-start(bf16[2304,8]{0,1:T(8,128)(2,1)} %param.17) | copy-start | bytes 110596
  76.3 4.5 %collective-permute-start = (bf16[3,8,1024]{2,1,0:T(8,128)(2,1)S(1)}, bf16[3,8,1024]{2,1,0:T(8,128)(2,1)S(1)}, u32[]{:S(2)}, u32[]{:S(2)}) collective-permute-start(bf16[3,8,1024]{2,1,0:T(8,128)(2,1)S(1)} %pad_maximum_fusion), channel_id=1, source_target_pairs={{0,4},{4,8},{8,12},{1,5},{5,9},{9,13},{2,6},{6,10},{10,14},{3,7},{... | collective-permute-start | bytes 147464 | tf_op jit(solution)/shard_map/ppermute | solution.py:161
  80.8 0.6 copy-start.4
  162.6 4.7 %collective-permute-start.1 = (bf16[8,128,128]{2,1,0:T(8,128)(2,1)S(1)}, bf16[8,128,128]{2,1,0:T(8,128)(2,1)S(1)}, u32[]{:S(2)}, u32[]{:S(2)}) collective-permute-start(bf16[8,128,128]{2,1,0:T(8,128)(2,1)S(1)} %slice.33), channel_id=1, source_target_pairs={{0,4},{4,8},{8,12},{1,5},{5,9},{9,13},{2,6},{6,10},{10,14},{3,7},{... | collective-permute-start | bytes 786440 | tf_op jit(solution)/shard_map/ppermute | solution.py:161
  168.8 5.8 %collective-permute-start.2 = (bf16[8,128,128]{2,1,0:T(8,128)(2,1)S(1)}, bf16[8,128,128]{2,1,0:T(8,128)(2,1)S(1)}, u32[]{:S(2)}, u32[]{:S(2)}) collective-permute-start(bf16[8,128,128]{2,1,0:T(8,128)(2,1)S(1)} %fusion), channel_id=1, source_target_pairs={{0,4},{4,8},{8,12},{1,5},{5,9},{9,13},{2,6},{6,10},{10,14},{3,7},{... | collective-permute-start | bytes 786440 | tf_op jit(solution)/shard_map/ppermute | solution.py:161
  176.1 7.7 %collective-permute-start.3 = (bf16[8,128,128]{2,1,0:T(8,128)(2,1)S(1)}, bf16[8,128,128]{2,1,0:T(8,128)(2,1)S(1)}, u32[]{:S(2)}, u32[]{:S(2)}) collective-permute-start(bf16[8,128,128]{2,1,0:T(8,128)(2,1)S(1)} %fusion.1), channel_id=1, source_target_pairs={{0,4},{4,8},{8,12},{1,5},{5,9},{9,13},{2,6},{6,10},{10,14},{3,7},{... | collective-permute-start | bytes 786440 | tf_op jit(solution)/shard_map/ppermute | solution.py:161
Sparse Core Ops, SparseCore 0:
  9.6 52.6 all-gather.3
  202.2 19.4 all-gather.5

commit v2 on v1

v2 whole, which is shorter than its diff:
```python
import functools
import math

import jax
import jax.numpy as jnp
from jax import lax
from jax.experimental import pallas as pl
from jax.experimental.pallas import tpu as pltpu
from jax.sharding import PartitionSpec as P

HALO = 16
MESH = pl.DeviceIdType.MESH
F32 = jnp.float32
BF16 = jnp.bfloat16
NT = (((1,), (1,)), ((), ()))
TN = (((0,), (0,)), ((), ()))


def dot(left, right, dims=None):
    left, right = left.astype(BF16), right.astype(BF16)
    if dims is None:
        return jnp.dot(left, right, preferred_element_type=F32)
    return lax.dot_general(left, right, dims, preferred_element_type=F32)


def softplus(value):
    return jnp.maximum(value, 0.0) + jnp.log1p(jnp.exp(-jnp.abs(value)))


def level_masks(chunk):
    row = lax.broadcasted_iota(jnp.int32, (chunk, chunk), 0)
    col = lax.broadcasted_iota(jnp.int32, (chunk, chunk), 1)
    masks = {}
    size = 1
    while size < chunk:
        differ = row ^ col
        masks[size] = (row > col) & (differ >= size) & (differ < 2 * size)
        size *= 2
    return row, col, masks


def level_reference(cum, size):
    chunk = cum.shape[0]
    if size >= 8:
        parts = cum.reshape(chunk // (2 * size), 2 * size, cum.shape[1])
        ref = parts[:, size - 1 : size, :]
        return jnp.broadcast_to(ref, parts.shape).reshape(cum.shape)
    parts = cum.reshape(chunk // 8, 8, cum.shape[1])
    place = lax.broadcasted_iota(jnp.int32, parts.shape, 1)
    ref = jnp.broadcast_to(parts[:, size - 1 : size, :], parts.shape)
    for start in range(2 * size, 8, 2 * size):
        ref = jnp.where(place >= start, parts[:, start + size - 1 : start + size, :], ref)
    return ref.reshape(cum.shape)


def copies_done(copies):
    for copy in copies:
        copy.wait()


def local_kernel(
    num_ctx, num_blocks,
    act_ref, wq_hbm, wk_hbm, wv_hbm, conv_ref, down_hbm, gu_ref, wb_ref, rate_ref, pos_ref,
    w_ref, u_ref, qk_ref, qup_ref, kend_ref, dec_ref, kf_ref, df_ref, dev_ref,
    buf, weights, down_ref, ext_ref, latent_ref, beta_ref,
    load_sem, own_sem, halo_send, halo_recv, right_sem, left_sem, recv_sem,
):
    chunk, width = act_ref.shape
    num_heads = rate_ref.shape[0]
    dim = gu_ref.shape[1] // num_heads
    group = min(4, num_heads)
    span = group * dim
    taps = conv_ref.shape[0]
    ctx, place = lax.axis_index("ctx"), lax.axis_index("head")
    rank = ctx * num_blocks + place
    ranks = num_ctx * num_blocks
    after, before = (rank + 1) % ranks, (rank + ranks - 1) % ranks
    next_id = {"ctx": after // num_blocks, "head": after % num_blocks}
    prev_id = {"ctx": before // num_blocks, "head": before % num_blocks}

    loads = [
        pltpu.make_async_copy(src, weights.at[j], load_sem.at[j])
        for j, src in enumerate((wq_hbm, wk_hbm, wv_hbm))
    ] + [pltpu.make_async_copy(down_hbm, down_ref, load_sem.at[3])]
    own = pltpu.make_async_copy(act_ref, buf.at[place, pl.ds(HALO, chunk)], own_sem)
    own.start()
    for copy in loads:
        copy.start()
    barrier = pltpu.get_barrier_semaphore()
    for other in (next_id, prev_id):
        pl.semaphore_signal(barrier, inc=1, device_id=other, device_id_type=MESH)
    pl.semaphore_wait(barrier, 2)
    halo = pltpu.make_async_remote_copy(
        src_ref=act_ref.at[pl.ds(chunk - HALO, HALO)],
        dst_ref=buf.at[after % num_blocks, pl.ds(0, HALO)],
        send_sem=halo_send, recv_sem=halo_recv, device_id=next_id, device_id_type=MESH,
    )
    halo.start()
    kf_ref[...] = jnp.zeros(kf_ref.shape, kf_ref.dtype)
    df_ref[...] = jnp.zeros(df_ref.shape, df_ref.dtype)
    own.wait()
    halo.wait()

    def to_right(i):
        block = jnp.maximum(place - i, 0)
        return pltpu.make_async_remote_copy(
            src_ref=buf.at[block], dst_ref=buf.at[block],
            send_sem=right_sem.at[i], recv_sem=recv_sem.at[block],
            device_id=next_id, device_id_type=MESH,
        )

    def to_left(i):
        block = jnp.minimum(place + i, num_blocks - 1)
        return pltpu.make_async_remote_copy(
            src_ref=buf.at[block], dst_ref=buf.at[block],
            send_sem=left_sem.at[i], recv_sem=recv_sem.at[block],
            device_id=prev_id, device_id_type=MESH,
        )

    def goes_right(i):
        return (place - i >= 0) & (place < num_blocks - 1) & (i < num_blocks - 1)

    def goes_left(i):
        return (place + i < num_blocks) & (place > 0) & (i < num_blocks - 1)

    row, col, masks = level_masks(chunk)
    eye = (row == col).astype(F32)
    tril = (row >= col).astype(BF16)
    heads = range(group)
    cut = lambda value, h: value[:, h * dim : (h + 1) * dim]

    def step(i, carry):
        @pl.when((i > 0) & (place - i >= 0))
        def _():
            to_right(i).wait_recv()

        @pl.when((i > 0) & (place + i < num_blocks))
        def _():
            to_left(i).wait_recv()

        @pl.when(goes_right(i))
        def _():
            to_right(i).start()

        @pl.when(goes_left(i))
        def _():
            to_left(i).start()

        @pl.when(i == 0)
        def _():
            copies_done(loads)

        over = (place + i) // num_blocks
        block = (place + i) * (1 - over) + (num_blocks - 1 - i) * over
        first_row = pl.multiple_of(block * chunk, chunk)
        rows = pl.ds(first_row, chunk)
        own_rows = buf[block, HALO:, :]
        latent_ref[...] = jnp.dot(own_rows, down_ref[...], preferred_element_type=F32).astype(BF16)
        beta_ref[...] = jnp.dot(own_rows, wb_ref[...], preferred_element_type=F32)
        halo_keep = jnp.where(ctx * num_blocks + block == 0, 0.0, 1.0).astype(F32)
        inner = pos_ref[0] - block * chunk
        here = (inner >= 0) & (inner < chunk)

        def head_group(hg, carry):
            cols = pl.ds(pl.multiple_of(hg * span, span), span)
            acts = []
            for j in range(3):
                proj = jnp.dot(buf[block], weights[j, :, cols], preferred_element_type=F32)
                proj = proj.astype(BF16).astype(F32)
                ext_ref[j, 0:HALO, :] = proj[:HALO] * halo_keep
                ext_ref[j, HALO:, :] = proj[HALO:]
                start = HALO + 1 - taps
                mixed = sum(
                    conv_ref[tap, j : j + 1, cols] * ext_ref[j, start + tap : start + tap + chunk, :]
                    for tap in range(taps)
                )
                acts.append(mixed / (1.0 + jnp.exp(-mixed)))

            def normed(value, factor):
                parts = []
                for h in heads:
                    part = cut(value, h)
                    total = jnp.sum(part * part, axis=-1, keepdims=True)
                    parts.append(part * (lax.rsqrt(total + 1e-06) * factor))
                return jnp.concatenate(parts, axis=1)

            query, key, value = normed(acts[0], 1.0 / math.sqrt(dim)), normed(acts[1], 1.0), acts[2]
            gate = softplus(jnp.dot(latent_ref[...], gu_ref[:, cols], preferred_element_type=F32))
            g = jnp.concatenate([cut(gate, h) * -rate_ref[hg * group + h] for h in heads], axis=1)
            lane = lax.broadcasted_iota(jnp.int32, beta_ref.shape, 1)
            betas = []
            for h in heads:
                pre = jnp.sum(jnp.where(lane == hg * group + h, beta_ref[...], 0.0), axis=1, keepdims=True)
                betas.append(1.0 / (1.0 + jnp.exp(-pre)))
            high = g.astype(BF16)
            low = (g - high.astype(F32)).astype(BF16)
            both = jnp.dot(tril, jnp.concatenate([high, low], axis=1), preferred_element_type=F32)
            cum = both[:, :span] + both[:, span:]
            product = query.astype(BF16).astype(F32) * key.astype(BF16).astype(F32)
            pair_k = [jnp.zeros((chunk, chunk), F32) for h in heads]
            pair_q = [
                jnp.where(row == col, jnp.sum(cut(product, h), axis=1, keepdims=True), 0.0) for h in heads
            ]
            for size, mask in masks.items():
                scale = jnp.exp(-jnp.abs(cum - level_reference(cum, size)))
                ks = (key * scale).astype(BF16)
                qs = (query * scale).astype(BF16)
                pairs = [
                    dot(jnp.concatenate([cut(ks, h), cut(qs, h)], axis=0), cut(ks, h), NT) for h in heads
                ]
                pair_k = [jnp.where(mask, p[:chunk], old) for p, old in zip(pairs, pair_k)]
                pair_q = [jnp.where(mask, p[chunk:], old) for p, old in zip(pairs, pair_q)]
            system = [betas[h] * pair_k[h] for h in heads]
            inverse = [eye - jnp.where(masks[1], system[h], 0.0) for h in heads]
            for size, mask in masks.items():
                if size > 1:
                    left = [dot(inverse[h], jnp.where(mask, system[h], 0.0)) for h in heads]
                    right = [dot(left[h], inverse[h]) for h in heads]
                    inverse = [inverse[h] - right[h] for h in heads]
            grown = jnp.exp(cum)
            key_up = key * grown
            last = cum[chunk - 1 : chunk, :]
            solved = [
                dot(inverse[h], jnp.concatenate([betas[h] * cut(value, h), betas[h] * cut(key_up, h)], axis=1))
                for h in heads
            ]
            u_ref[rows, cols] = jnp.concatenate([s[:, :dim] for s in solved], axis=1)
            w_ref[rows, cols] = jnp.concatenate([s[:, dim:] for s in solved], axis=1).astype(BF16)
            for h in heads:
                qk_ref[hg * group + h, rows, :] = pair_q[h].astype(BF16)
            qup_ref[rows, cols] = (query * grown).astype(BF16)
            kend_ref[rows, cols] = (key * jnp.exp(last - cum)).astype(BF16)
            whole = jnp.exp(last)
            at = jnp.sum(jnp.where(row[:, :1] == inner, cum, 0.0), axis=0, keepdims=True)
            keep = (row[:, :1] <= inner) & here
            kf_new = jnp.where(keep, key * jnp.exp(jnp.minimum(at - cum, 0.0)), 0.0)
            df_new = jnp.where(here, jnp.exp(at), 0.0)
            for h in heads:
                dec_ref[hg * group + h, pl.ds(block, 1), :] = cut(whole, h)
                kf_ref[hg * group + h] += cut(kf_new, h).astype(BF16)
                df_ref[hg * group + h] += jnp.broadcast_to(cut(df_new, h), (8, dim))
            return carry

        return lax.fori_loop(0, num_heads // group, head_group, carry)

    lax.fori_loop(0, num_blocks, step, 0)

    def compose(hg, carry):
        stacked = [jnp.concatenate([jnp.eye(dim, dtype=F32), jnp.zeros((dim, dim), F32)], axis=0) for h in heads]
        for c in range(num_blocks):
            rows = slice(c * chunk, (c + 1) * chunk)
            head_cols = [pl.ds(pl.multiple_of((hg * group + h) * dim, dim), dim) for h in heads]
            change = [
                jnp.concatenate([jnp.zeros((chunk, dim), F32), u_ref[rows, head_cols[h]]], axis=1)
                - dot(w_ref[rows, head_cols[h]], stacked[h], NT)
                for h in heads
            ]
            stacked = [
                stacked[h] * dec_ref[hg * group + h, c : c + 1, :]
                + dot(change[h], kend_ref[rows, head_cols[h]], TN)
                for h in heads
            ]
        for h in heads:
            dev_ref[hg * group + h] = stacked[h]
        return carry

    lax.fori_loop(0, num_heads // group, compose, 0)

    def drain(i, carry):
        @pl.when(goes_right(i))
        def _():
            to_right(i).wait_send()

        @pl.when(goes_left(i))
        def _():
            to_left(i).wait_send()

        return carry

    lax.fori_loop(0, num_blocks - 1, drain, 0)


def read_kernel(
    start_ref, w_ref, u_ref, qk_ref, qup_ref, kend_ref, dec_ref, kf_ref, df_ref, pos_ref,
    out_ref, fork_ref,
):
    seq_len, dim = w_ref.shape
    chunk = seq_len // dec_ref.shape[1]
    state = start_ref[0]
    pos = pos_ref[0]
    fork_ref[0] = jnp.zeros((dim, dim), BF16)
    for c in range(seq_len // chunk):
        rows = slice(c * chunk, (c + 1) * chunk)
        both = dot(jnp.concatenate([w_ref[rows, :], qup_ref[rows, :]], axis=0), state, NT)
        change = (u_ref[rows, :] - both[:chunk]).astype(BF16)
        out_ref[rows, :] = (both[chunk:] + dot(qk_ref[0, rows, :], change)).astype(BF16)

        @pl.when((pos >= c * chunk) & (pos < (c + 1) * chunk))
        def _():
            saved = state * df_ref[0, 0:1, :] + dot(change, kf_ref[0], TN)
            fork_ref[0] = saved.T.astype(BF16)

        state = state * dec_ref[0, c : c + 1, :] + dot(change, kend_ref[rows, :], TN)


def shifted(value, axis, by):
    size = lax.axis_size(axis)
    pairs = [(i, i + by) for i in range(size) if 0 <= i + by < size]
    return lax.ppermute(value, axis, pairs)


def per_device(
    activations, w_query, w_key, w_value, conv_weight, gate_down, gate_up, w_beta, decay_rate, fork_pos
):
    chunk, width = activations.shape
    num_blocks = lax.axis_size("head")
    seq_len = chunk * num_blocks
    num_heads = w_beta.shape[1]
    head_cols = w_query.shape[1]
    dim = head_cols // num_heads
    num_ctx = lax.axis_size("ctx")
    num_forks = fork_pos.shape[0]
    per_fork = num_ctx // num_forks
    ctx = lax.axis_index("ctx")
    pos = lax.dynamic_slice(fork_pos, (ctx // per_fork,), (1,)) - ctx * seq_len
    span = min(4, num_heads) * dim

    column = pl.BlockSpec((seq_len, dim), lambda h: (0, h))
    per_head = lambda *shape: pl.BlockSpec((1,) + shape, lambda h: (h,) + (0,) * len(shape))
    smem = pl.BlockSpec(memory_space=pltpu.SMEM)
    vmem = pl.BlockSpec(memory_space=pltpu.VMEM)
    hbm = pl.BlockSpec(memory_space=pl.ANY)
    cols = lambda dtype: jax.ShapeDtypeStruct((seq_len, head_cols), dtype)
    heads = lambda dtype, *shape: jax.ShapeDtypeStruct((num_heads,) + shape, dtype)
    w, u, qk, qup, kend, dec, kf, df, dev = pl.pallas_call(
        functools.partial(local_kernel, num_ctx, num_blocks),
        in_specs=[vmem, hbm, hbm, hbm, vmem, hbm, vmem, vmem, smem, smem],
        out_specs=[vmem] * 9,
        out_shape=[
            cols(BF16), cols(F32), heads(BF16, seq_len, chunk), cols(BF16), cols(BF16),
            heads(F32, num_blocks, dim), heads(BF16, chunk, dim), heads(F32, 8, dim), heads(F32, 2 * dim, dim),
        ],
        scratch_shapes=[
            pltpu.VMEM((num_blocks, HALO + chunk, width), BF16),
            pltpu.VMEM((3, width, head_cols), BF16),
            pltpu.VMEM((width, gate_down.shape[1]), BF16),
            pltpu.VMEM((3, HALO + chunk, span), F32),
            pltpu.VMEM((chunk, gate_down.shape[1]), BF16),
            pltpu.VMEM((chunk, num_heads), F32),
            pltpu.SemaphoreType.DMA((4,)),
            pltpu.SemaphoreType.DMA,
            pltpu.SemaphoreType.DMA,
            pltpu.SemaphoreType.DMA,
            pltpu.SemaphoreType.DMA((num_blocks,)),
            pltpu.SemaphoreType.DMA((num_blocks,)),
            pltpu.SemaphoreType.DMA((num_blocks,)),
        ],
        compiler_params=pltpu.CompilerParams(
            collective_id=0, has_side_effects=True, vmem_limit_bytes=60 << 20
        ),
        name="local",
    )(activations, w_query, w_key, w_value, conv_weight, gate_down, gate_up, w_beta, decay_rate, pos)

    trans, offset = dev[:, :dim], dev[:, dim:]
    start = jnp.zeros((num_heads, dim, dim), F32)
    for turn in range(num_ctx - 1):
        end = offset if turn == 0 else offset + jnp.einsum(
            "hij,hjk->hik", start, trans, precision=lax.Precision.HIGH
        )
        start = shifted(end.astype(BF16), "ctx", 1).astype(F32)

    attended, fork_local = pl.pallas_call(
        read_kernel,
        grid=(num_heads,),
        in_specs=[
            per_head(dim, dim), column, column, per_head(seq_len, chunk), column, column,
            per_head(num_blocks, dim), per_head(chunk, dim), per_head(8, dim), smem,
        ],
        out_specs=[column, per_head(dim, dim)],
        out_shape=[cols(BF16), heads(BF16, dim, dim)],
        name="read",
    )(start, w, u, qk, qup, kend, dec, kf, df, pos)
    everyone = lax.all_gather(fork_local, "ctx", axis=0)
    fork_states = everyone.reshape((num_forks, per_fork) + fork_local.shape).astype(F32).sum(axis=1)
    return attended, fork_states


def solution(mesh):
    return jax.shard_map(
        per_device,
        mesh=mesh,
        in_specs=(
            P(("group", "ctx", "head"), None),
            P(None, "head"),
            P(None, "head"),
            P(None, "head"),
            P(None, None, "head"),
            P(),
            P(None, "head"),
            P(None, "head"),
            P("head"),
            P("group"),
        ),
        out_specs=(P(("group", "ctx"), "head"), P("group", "head", None, None)),
        check_vma=False,
    )
```

time: 232 us -> 156 us (0.67)
  waiting for transfers between devices: 74.7 us -> 23.1 us
  matrix products: 19.7 us -> 2.99 us
  Pallas kernels: 97.6 us -> 91.6 us
    all_gather x1 -> x0, waiting for transfers between devices: 51 us -> none  [per_device(): gathered = lax.all_gather(activations, 'head', axis=0, tiled=True)]
    dot_general x5 -> x0, matrix products: 16.7 us -> none  [the longest x3 13.8 us: per_device(): jnp.dot(gathered, weights, preferred_element_type=F32).astype(BF16)]
    pallas_call x1, Pallas kernels: 80.1 us -> 74.1 us  [per_device(): pl.pallas_call(functools.partial(local_kernel, num_ctx, num_blocks), in_s...]
    ppermute x4 -> x3, starting transfers between devices: 16.3 us -> 14.7 us  [shifted(): return lax.ppermute(value, axis, pairs)]
  transfers between devices with their start and end apart: 6 -> 4, of which waited for: 5 -> 4; matrix products, arithmetic and copies ran while one was open for 2% -> 0% of each run, Pallas kernels for 0% -> 0%
where the time goes in v2:
time: 156 us
  Pallas kernels  91.6 us (59%)
  waiting for transfers between devices  23.1 us (15%)
  starting transfers between devices  14.7 us (9%)
  between operations  14.7 us (9%)
  local copies, waits for them, and re-layouts  5.6 us (4%)
  other arithmetic  3.3 us (2%)
  matrix products  2.99 us (2%)
    pallas_call x1, Pallas kernels, per_device(): pl.pallas_call(functools.partial(local_kernel, num_ctx, num_blocks), in_s...  74.1 us
    all_gather x1, waiting for transfers between devices, per_device(): everyone = lax.all_gather(fork_local, 'ctx', axis=0)  19.7 us
    pallas_call x1, Pallas kernels, per_device(): pl.pallas_call(read_kernel, grid=(num_heads,), in_specs=[per_head(dim, di...  17.5 us
    ppermute x3, starting transfers between devices, shifted(): return lax.ppermute(value, axis, pairs)  14.7 us
    ppermute x3, waiting for transfers between devices, shifted(): return lax.ppermute(value, axis, pairs)  3.39 us
    unnamed x2, local copies, waits for them, and re-layouts  3.29 us
  transfers between devices with their start and end apart: 4, of which 4 were waited for; matrix products, arithmetic and copies ran while one was open for 0% of the time, Pallas kernels for 0%

profile of v2, /device:TPU:0, one launch (start us, length us, event | category | flops | bytes accessed | tf_op | source)
XLA Modules:
  0.0 156.0 jit_solution(9119166911874589579)
XLA Ops:
  7.2 0.0 all-gather.3.cloned.1.call-start
  7.2 1.5 copy.14.conv_ref
  8.7 1.8 %copy.15.wb_ref = bf16[2304,8]{1,0:T(8,128)(2,1)} copy(bf16[2304,8]{0,1:T(8,128)(2,1)} %param.17) | data formatting | bytes 73728 | tf_op args[7]
  10.5 1.2 dynamic_slice.3
  12.3 74.1 %local.1 = (bf16[512,1024]{1,0:T(8,128)(2,1)}, f32[512,1024]{1,0:T(8,128)}, bf16[8,512,128]{2,1,0:T(8,128)(2,1)}, bf16[512,1024]{1,0:T(8,128)(2,1)}, bf16[512,10...) custom-call(bf16[128,2304]{1,0:T(8,128)(2,1)} %act_ref.1, ...), custom_call_target="tpu_custom_call" | custom-call | tf_op jit(solution)/shard_map/local/pallas_call | solution.py:335
  86.5 1.1 slice.15
  87.5 1.5 collective-permute-start
  89.0 1.1 collective-permute-done
  90.1 1.5 fusion
  91.6 6.6 %collective-permute-start.1 = (bf16[8,128,128]{2,1,0:T(8,128)(2,1)S(1)}, bf16[8,128,128]{2,1,0:T(8,128)(2,1)S(1)}, u32[]{:S(2)}, u32[]{:S(2)}) collective-permute-start(bf16[8,128,128]{2,1,0:T(8,128)(2,1)S(1)} %fusion), channel_id=1, source_target_pairs={{0,4},{4,8},{8,12},{1,5},{5,9},{9,13},{2,6},{6,10},{10,14},{3,7},{... | collective-permute-start | bytes 786440 | tf_op jit(solution)/shard_map/ppermute | solution.py:309
  98.3 1.1 collective-permute-done.1
  99.4 1.5 fusion.1
  100.9 6.6 %collective-permute-start.2 = (bf16[8,128,128]{2,1,0:T(8,128)(2,1)S(1)}, bf16[8,128,128]{2,1,0:T(8,128)(2,1)S(1)}, u32[]{:S(2)}, u32[]{:S(2)}) collective-permute-start(bf16[8,128,128]{2,1,0:T(8,128)(2,1)S(1)} %fusion.1), channel_id=1, source_target_pairs={{0,4},{4,8},{8,12},{1,5},{5,9},{9,13},{2,6},{6,10},{10,14},{3,7},{... | collective-permute-start | bytes 786440 | tf_op jit(solution)/shard_map/ppermute | solution.py:309
  107.5 1.1 collective-permute-done.2
  108.6 0.8 convert_element_type.23.start_ref
  109.4 17.5 %read.1 = (bf16[512,1024]{1,0:T(8,128)(2,1)}, bf16[8,128,128]{2,1,0:T(8,128)(2,1)}) custom-call(f32[8,128,128]{2,1,0:T(8,128)} %convert_element_type.23.start_ref, bf16[512,1024]{1,0:T(8,128)(2,1)} %get-tuple-element.14.w_ref, f32[512,1024]{1,0:T(8,128)} %get-tuple-element.15.u_ref, bf16[8,512,128]{2,1,0:T(8,128)(2,1)} %get-tuple-element.16.qk_ref, ...), custom_call_target="tpu_custom_call" | custom-call | tf_op jit(solution)/shard_map/read/pallas_call | solution.py:372
  126.9 0.0 all-gather.3.cloned.1.call-update
  127.0 19.7 %all-gather.3.cloned.1.call-done = bf16[32,128,128]{2,1,0:T(8,128)(2,1)} async-done(((bf16[8,128,128]{2,1,0:T(8,128)(2,1)}), bf16[32,128,128]{2,1,0:T(8,128)(2,1)}) %all-gather.3.cloned.1.call-update) | async-done | bytes 1048592 | tf_op jit(solution)/shard_map/all_gather | solution.py:383
  146.7 2.5 %convert_reduce_fusion = f32[2,8,128,128]{3,2,1,0:T(8,128)} fusion(bf16[2,2,8,128,128]{4,3,2,1,0:T(8,128)(2,1)} %bitcast.5), kind=kLoop, calls=%fused_computation | loop fusion | flops 786432 | bytes 2097152 | tf_op jit(solution)/shard_map/reduce_sum | solution.py:384
Async XLA Ops:
  7.2 139.5 %all-gather.3.cloned.1.call-start = ((), (), s32[]{:S(2)}) async-start(), calls=%async_computation | async-start | bytes 1310720 | tf_op jit(solution)/shard_map/all_gather | solution.py:383
  87.5 2.6 %collective-permute-start = (bf16[8,128,128]{2,1,0:T(8,128)(2,1)S(1)}, bf16[8,128,128]{2,1,0:T(8,128)(2,1)S(1)}, u32[]{:S(2)}, u32[]{:S(2)}) collective-permute-start(bf16[8,128,128]{2,1,0:T(8,128)(2,1)S(1)} %slice.15), channel_id=1, source_target_pairs={{0,4},{4,8},{8,12},{1,5},{5,9},{9,13},{2,6},{6,10},{10,14},{3,7},{... | collective-permute-start | bytes 786440 | tf_op jit(solution)/shard_map/ppermute | solution.py:309
  91.6 7.8 %collective-permute-start.1 = (bf16[8,128,128]{2,1,0:T(8,128)(2,1)S(1)}, bf16[8,128,128]{2,1,0:T(8,128)(2,1)S(1)}, u32[]{:S(2)}, u32[]{:S(2)}) collective-permute-start(bf16[8,128,128]{2,1,0:T(8,128)(2,1)S(1)} %fusion), channel_id=1, source_target_pairs={{0,4},{4,8},{8,12},{1,5},{5,9},{9,13},{2,6},{6,10},{10,14},{3,7},{... | collective-permute-start | bytes 786440 | tf_op jit(solution)/shard_map/ppermute | solution.py:309
  100.9 7.7 %collective-permute-start.2 = (bf16[8,128,128]{2,1,0:T(8,128)(2,1)S(1)}, bf16[8,128,128]{2,1,0:T(8,128)(2,1)S(1)}, u32[]{:S(2)}, u32[]{:S(2)}) collective-permute-start(bf16[8,128,128]{2,1,0:T(8,128)(2,1)S(1)} %fusion.1), channel_id=1, source_target_pairs={{0,4},{4,8},{8,12},{1,5},{5,9},{9,13},{2,6},{6,10},{10,14},{3,7},{... | collective-permute-start | bytes 786440 | tf_op jit(solution)/shard_map/ppermute | solution.py:309
Sparse Core Ops, SparseCore 0:
  127.1 19.5 all-gather.2

commit v3 on v2

--- a/solution.py
+++ b/solution.py
@@ -61,9 +61,13 @@
 def local_kernel(
     num_ctx, num_blocks,
     act_ref, wq_hbm, wk_hbm, wv_hbm, conv_ref, down_hbm, gu_ref, wb_ref, rate_ref, pos_ref,
-    w_ref, u_ref, qk_ref, qup_ref, kend_ref, dec_ref, kf_ref, df_ref, dev_ref,
+    out_ref, forks_ref,
+    w_ref, u_ref, qk_ref, qup_ref, kend_ref, dec_ref, kf_ref, df_ref,
+    prefix_ref, change_ref, dev_ref, gain_ref, base_ref, fork_gain, fork_base,
+    start_ref, end_ref, part_ref, other_ref, fork_ref,
     buf, weights, down_ref, ext_ref, latent_ref, beta_ref,
     load_sem, own_sem, halo_send, halo_recv, right_sem, left_sem, recv_sem,
+    chain_send, chain_recv, pair_send, pair_recv, fork_send, fork_recv,
 ):
     chunk, width = act_ref.shape
     num_heads = rate_ref.shape[0]
@@ -89,7 +93,11 @@
     barrier = pltpu.get_barrier_semaphore()
     for other in (next_id, prev_id):
         pl.semaphore_signal(barrier, inc=1, device_id=other, device_id_type=MESH)
-    pl.semaphore_wait(barrier, 2)
+    for turn in range(1, num_ctx):
+        pl.semaphore_signal(
+            barrier, inc=1, device_id={"ctx": (ctx + turn) % num_ctx}, device_id_type=MESH
+        )
+    pl.semaphore_wait(barrier, num_ctx + 1)
     halo = pltpu.make_async_remote_copy(
         src_ref=act_ref.at[pl.ds(chunk - HALO, HALO)],
         dst_ref=buf.at[after % num_blocks, pl.ds(0, HALO)],
@@ -251,10 +259,15 @@
             rows = slice(c * chunk, (c + 1) * chunk)
             head_cols = [pl.ds(pl.multiple_of((hg * group + h) * dim, dim), dim) for h in heads]
             change = [
-                jnp.concatenate([jnp.zeros((chunk, dim), F32), u_ref[rows, head_cols[h]]], axis=1)
-                - dot(w_ref[rows, head_cols[h]], stacked[h], NT)
+                (
+                    jnp.concatenate([jnp.zeros((chunk, dim), F32), u_ref[rows, head_cols[h]]], axis=1)
+                    - dot(w_ref[rows, head_cols[h]], stacked[h], NT)
+                ).astype(BF16)
                 for h in heads
             ]
+            for h in heads:
+                prefix_ref[hg * group + h, c] = stacked[h]
+                change_ref[hg * group + h, c] = change[h]
             stacked = [
                 stacked[h] * dec_ref[hg * group + h, c : c + 1, :]
                 + dot(change[h], kend_ref[rows, head_cols[h]], TN)
@@ -264,7 +277,116 @@
             dev_ref[hg * group + h] = stacked[h]
         return carry
 
-    lax.fori_loop(0, num_heads // group, compose, 0)
+    groups = num_heads // group
+    lax.fori_loop(0, groups, compose, 0)
+
+    @pl.when(ctx == 0)
+    def _():
+        start_ref[...] = jnp.zeros(start_ref.shape, BF16)
+
+    def pass_on(gi):
+        part = pl.ds(gi * group, group)
+        return pltpu.make_async_remote_copy(
+            src_ref=end_ref.at[part], dst_ref=start_ref.at[part],
+            send_sem=chain_send.at[gi], recv_sem=chain_recv.at[gi],
+            device_id={"ctx": jnp.minimum(ctx + 1, num_ctx - 1)}, device_id_type=MESH,
+        )
+
+    def chain():
+        def one(gi, carry):
+            @pl.when(ctx > 0)
+            def _():
+                pass_on(gi).wait_recv()
+
+            @pl.when(ctx < num_ctx - 1)
+            def _():
+                ends = []
+                for h in heads:
+                    trans = dev_ref[gi * group + h, :dim, :]
+                    fine = (trans - trans.astype(BF16).astype(F32)).astype(BF16)
+                    first = start_ref[gi * group + h]
+                    ends.append(dot(first, trans) + dot(first, fine) + dev_ref[gi * group + h, dim:, :])
+                for h in heads:
+                    end_ref[gi * group + h] = ends[h].astype(BF16)
+                pass_on(gi).start()
+
+            return carry
+
+        lax.fori_loop(0, groups, one, 0)
+
+    pair = 2
+    which = pos_ref[1]
+    owned = (pos_ref[0] >= 0) & (pos_ref[0] < num_blocks * chunk)
+
+    def read(j, carry):
+        @pl.when(ctx == j)
+        def _():
+            chain()
+
+        for p in range(pair):
+            h = j * pair + p
+            cols = pl.ds(pl.multiple_of(h * dim, dim), dim)
+            for c in range(num_blocks):
+                rows = slice(c * chunk, (c + 1) * chunk)
+                both = dot(qup_ref[rows, cols], prefix_ref[h, c], NT) + dot(qk_ref[h, rows, :], change_ref[h, c])
+                gain_ref[rows, cols] = both[:, :dim].astype(BF16)
+                base_ref[rows, cols] = both[:, dim:]
+            saved = prefix_ref[h, which] * df_ref[h, 0:1, :] + dot(change_ref[h, which], kf_ref[h], TN)
+            fork_gain[h] = saved[:dim].T.astype(BF16)
+            fork_base[h] = saved[dim:].T
+        return carry
+
+    parts = num_heads // pair
+    lax.fori_loop(0, parts, read, 0)
+
+    @pl.when(ctx >= parts)
+    def _():
+        chain()
+
+    half = num_heads // 2
+    core = ctx % 2
+    mine = ctx // 2
+
+    for h in range(num_heads):
+        state = fork_base[h] + dot(fork_gain[h], start_ref[h], NT)
+        part_ref[h] = jnp.where(owned, state, 0.0).astype(BF16)
+    swap = pltpu.make_async_remote_copy(
+        src_ref=part_ref.at[pl.ds((1 - core) * half, half)], dst_ref=other_ref,
+        send_sem=pair_send, recv_sem=pair_recv,
+        device_id={"ctx": mine * 2 + 1 - core}, device_id_type=MESH,
+    )
+    swap.start()
+
+    def finish(h, carry):
+        cols = pl.ds(pl.multiple_of(h * dim, dim), dim)
+        out_ref[:, cols] = (base_ref[:, cols] + dot(gain_ref[:, cols], start_ref[h], NT)).astype(BF16)
+        return carry
+
+    lax.fori_loop(0, half, finish, 0)
+    swap.wait()
+    own_half = pl.ds(core * half, half)
+    fork_ref[mine, own_half] = (part_ref[own_half].astype(F32) + other_ref[...].astype(F32)).astype(BF16)
+
+    def share(turn, source):
+        block = fork_ref.at[source // 2, pl.ds((source % 2) * half, half)]
+        return pltpu.make_async_remote_copy(
+            src_ref=block, dst_ref=block,
+            send_sem=fork_send.at[turn], recv_sem=fork_recv.at[source],
+            device_id={"ctx": (ctx + turn) % num_ctx}, device_id_type=MESH,
+        )
+
+    for turn in range(1, num_ctx):
+        share(turn, ctx).start()
+    lax.fori_loop(half, num_heads, finish, 0)
+    for turn in range(1, num_ctx):
+        share(turn, (ctx + turn) % num_ctx).wait_recv()
+    for turn in range(1, num_ctx):
+        share(turn, ctx).wait_send()
+    forks_ref[...] = fork_ref[...].astype(F32)
+
+    @pl.when(ctx < num_ctx - 1)
+    def _():
+        lax.fori_loop(0, groups, lambda gi, carry: (pass_on(gi).wait_send(), carry)[1], 0)
 
     def drain(i, carry):
         @pl.when(goes_right(i))
@@ -278,35 +400,6 @@
         return carry
 
     lax.fori_loop(0, num_blocks - 1, drain, 0)
-
-
-def read_kernel(
-    start_ref, w_ref, u_ref, qk_ref, qup_ref, kend_ref, dec_ref, kf_ref, df_ref, pos_ref,
-    out_ref, fork_ref,
-):
-    seq_len, dim = w_ref.shape
-    chunk = seq_len // dec_ref.shape[1]
-    state = start_ref[0]
-    pos = pos_ref[0]
-    fork_ref[0] = jnp.zeros((dim, dim), BF16)
-    for c in range(seq_len // chunk):
-        rows = slice(c * chunk, (c + 1) * chunk)
-        both = dot(jnp.concatenate([w_ref[rows, :], qup_ref[rows, :]], axis=0), state, NT)
-        change = (u_ref[rows, :] - both[:chunk]).astype(BF16)
-        out_ref[rows, :] = (both[chunk:] + dot(qk_ref[0, rows, :], change)).astype(BF16)
-
-        @pl.when((pos >= c * chunk) & (pos < (c + 1) * chunk))
-        def _():
-            saved = state * df_ref[0, 0:1, :] + dot(change, kf_ref[0], TN)
-            fork_ref[0] = saved.T.astype(BF16)
-
-        state = state * dec_ref[0, c : c + 1, :] + dot(change, kend_ref[rows, :], TN)
-
-
-def shifted(value, axis, by):
-    size = lax.axis_size(axis)
-    pairs = [(i, i + by) for i in range(size) if 0 <= i + by < size]
-    return lax.ppermute(value, axis, pairs)
 
 
 def per_device(
@@ -322,25 +415,33 @@
     num_forks = fork_pos.shape[0]
     per_fork = num_ctx // num_forks
     ctx = lax.axis_index("ctx")
+    assert per_fork == 2 and num_heads % 2 == 0
     pos = lax.dynamic_slice(fork_pos, (ctx // per_fork,), (1,)) - ctx * seq_len
+    pos = jnp.concatenate([pos, jnp.clip(pos, 0, seq_len - 1) // chunk])
     span = min(4, num_heads) * dim
 
-    column = pl.BlockSpec((seq_len, dim), lambda h: (0, h))
-    per_head = lambda *shape: pl.BlockSpec((1,) + shape, lambda h: (h,) + (0,) * len(shape))
     smem = pl.BlockSpec(memory_space=pltpu.SMEM)
     vmem = pl.BlockSpec(memory_space=pltpu.VMEM)
     hbm = pl.BlockSpec(memory_space=pl.ANY)
-    cols = lambda dtype: jax.ShapeDtypeStruct((seq_len, head_cols), dtype)
-    heads = lambda dtype, *shape: jax.ShapeDtypeStruct((num_heads,) + shape, dtype)
-    w, u, qk, qup, kend, dec, kf, df, dev = pl.pallas_call(
+    cols = lambda dtype: pltpu.VMEM((seq_len, head_cols), dtype)
+    heads = lambda dtype, *shape: pltpu.VMEM((num_heads,) + shape, dtype)
+    return pl.pallas_call(
         functools.partial(local_kernel, num_ctx, num_blocks),
         in_specs=[vmem, hbm, hbm, hbm, vmem, hbm, vmem, vmem, smem, smem],
-        out_specs=[vmem] * 9,
+        out_specs=[vmem] * 2,
         out_shape=[
-            cols(BF16), cols(F32), heads(BF16, seq_len, chunk), cols(BF16), cols(BF16),
-            heads(F32, num_blocks, dim), heads(BF16, chunk, dim), heads(F32, 8, dim), heads(F32, 2 * dim, dim),
+            jax.ShapeDtypeStruct((seq_len, head_cols), BF16),
+            jax.ShapeDtypeStruct((num_forks, num_heads, dim, dim), F32),
         ],
         scratch_shapes=[
+            cols(BF16), cols(F32), heads(BF16, seq_len, chunk), cols(BF16), cols(BF16),
+            heads(F32, num_blocks, dim), heads(BF16, chunk, dim), heads(F32, 8, dim),
+            heads(F32, num_blocks, 2 * dim, dim), heads(BF16, num_blocks, chunk, 2 * dim),
+            heads(F32, 2 * dim, dim), cols(BF16), cols(F32),
+            heads(BF16, dim, dim), heads(F32, dim, dim),
+            heads(BF16, dim, dim), heads(BF16, dim, dim), heads(BF16, dim, dim),
+            pltpu.VMEM((num_heads // 2, dim, dim), BF16),
+            pltpu.VMEM((num_forks, num_heads, dim, dim), BF16),
             pltpu.VMEM((num_blocks, HALO + chunk, width), BF16),
             pltpu.VMEM((3, width, head_cols), BF16),
             pltpu.VMEM((width, gate_down.shape[1]), BF16),
@@ -354,35 +455,18 @@
             pltpu.SemaphoreType.DMA((num_blocks,)),
             pltpu.SemaphoreType.DMA((num_blocks,)),
             pltpu.SemaphoreType.DMA((num_blocks,)),
+            pltpu.SemaphoreType.DMA((num_heads // min(4, num_heads),)),
+            pltpu.SemaphoreType.DMA((num_heads // min(4, num_heads),)),
+            pltpu.SemaphoreType.DMA,
+            pltpu.SemaphoreType.DMA,
+            pltpu.SemaphoreType.DMA((num_ctx,)),
+            pltpu.SemaphoreType.DMA((num_ctx,)),
         ],
         compiler_params=pltpu.CompilerParams(
             collective_id=0, has_side_effects=True, vmem_limit_bytes=60 << 20
         ),
         name="local",
     )(activations, w_query, w_key, w_value, conv_weight, gate_down, gate_up, w_beta, decay_rate, pos)
-
-    trans, offset = dev[:, :dim], dev[:, dim:]
-    start = jnp.zeros((num_heads, dim, dim), F32)
-    for turn in range(num_ctx - 1):
-        end = offset if turn == 0 else offset + jnp.einsum(
-            "hij,hjk->hik", start, trans, precision=lax.Precision.HIGH
-        )
-        start = shifted(end.astype(BF16), "ctx", 1).astype(F32)
-
-    attended, fork_local = pl.pallas_call(
-        read_kernel,
-        grid=(num_heads,),
-        in_specs=[
-            per_head(dim, dim), column, column, per_head(seq_len, chunk), column, column,
-            per_head(num_blocks, dim), per_head(chunk, dim), per_head(8, dim), smem,
-        ],
-        out_specs=[column, per_head(dim, dim)],
-        out_shape=[cols(BF16), heads(BF16, dim, dim)],
-        name="read",
-    )(start, w, u, qk, qup, kend, dec, kf, df, pos)
-    everyone = lax.all_gather(fork_local, "ctx", axis=0)
-    fork_states = everyone.reshape((num_forks, per_fork) + fork_local.shape).astype(F32).sum(axis=1)
-    return attended, fork_states
 
 
 def solution(mesh):

time: 156 us -> 101 us (0.65); the launches traced: 156 us -> 99.2 us
  waiting for transfers between devices: 23.1 us -> 0 us
  starting transfers between devices: 14.7 us -> 0 us
  between operations: 14.7 us -> 1.32 us
  local copies, waits for them, and re-layouts: 5.6 us -> 9.09 us
  Pallas kernels: 91.6 us -> 88.2 us
  matrix products: 2.99 us -> 0 us
  other arithmetic: 3.3 us -> 0.62 us
    all_gather x1 -> x0, waiting for transfers between devices: 19.7 us -> none  [per_device(): everyone = lax.all_gather(fork_local, 'ctx', axis=0)]
    pallas_call x1 -> x0, Pallas kernels: 17.5 us -> none  [per_device(): pl.pallas_call(read_kernel, grid=(num_heads,), in_specs=[per_head(dim, di...]
    ppermute x3 -> x0, starting transfers between devices: 14.7 us -> none  [shifted(): return lax.ppermute(value, axis, pairs)]
    pallas_call x1, Pallas kernels: 74.1 us -> 88.2 us  [per_device(): pl.pallas_call(functools.partial(local_kernel, num_ctx, num_blocks), in_s...]
    unnamed x2 -> x4, local copies, waits for them, and re-layouts: 3.29 us -> 7.84 us
    ppermute x3 -> x0, waiting for transfers between devices: 3.39 us -> none  [shifted(): return lax.ppermute(value, axis, pairs)]
    dot_general x2 -> x0, matrix products: 2.99 us -> none  [per_device(): jnp.einsum('hij,hjk->hik', start, trans, precision=lax.Precision.HIGH)]
    reduce_sum x1 -> x0, other arithmetic: 2.47 us -> none  [per_device(): everyone.reshape((num_forks, per_fork) + fork_local.shape).astype(F32)]
  transfers between devices with their start and end apart: 4 -> 0, of which waited for: 4 -> 0; matrix products, arithmetic and copies ran while one was open for 0% -> 0% of each run, Pallas kernels for 0% -> 0%
where the time goes in v3:
time: 101 us; the launch traced here: 99.2 us
  Pallas kernels  88.2 us (87%)
  local copies, waits for them, and re-layouts  9.09 us (9%)
  between operations  1.32 us (1%)
    pallas_call x1, Pallas kernels, per_device(): pl.pallas_call(functools.partial(local_kernel, num_ctx, num_blocks), in_s...  88.2 us
    unnamed x4, local copies, waits for them, and re-layouts  7.84 us

profile of v3, /device:TPU:0, one launch (start us, length us, event | category | flops | bytes accessed | tf_op | source)
XLA Modules:
  0.0 99.2 jit_solution(2013670785070620039)
XLA Ops:
  0.6 1.2 %dynamic_slice.3 = s32[1]{0:T(128)} dynamic-slice(s32[2]{0:T(128)} %param.19, s32[]{:T(128)S(6)} %select_n.14), dynamic_slice_sizes={1} | dynamic-slice | bytes 12 | tf_op jit(solution)/shard_map/dynamic_slice | solution.py:419
  2.6 0.6 pad_add_fusion.pos_ref
  3.2 1.5 %copy.12.conv_ref = f32[4,3,1024]{2,1,0:T(4,128)} copy(f32[4,3,1024]{2,0,1:T(4,128)} %param.14) | data formatting | bytes 98304 | tf_op args[4]
  4.6 1.8 %copy.13.wb_ref = bf16[2304,8]{1,0:T(8,128)(2,1)} copy(bf16[2304,8]{0,1:T(8,128)(2,1)} %param.17) | data formatting | bytes 73728 | tf_op args[7]
  6.5 88.2 %local.1 = (bf16[512,1024]{1,0:T(8,128)(2,1)}, f32[2,8,128,128]{3,2,1,0:T(8,128)}) custom-call(bf16[128,2304]{1,0:T(8,128)(2,1)} %act_ref.1, bf16[2304,1024]{1,0:T(8,128)(2,1)} %wq_hbm.1, bf16[2304,1024]{1,0:T(8,128)(2,1)} %wk_hbm.1, bf16[2304,1024]{1,0:T(8,128)(2,1)} %wv_hbm.1, f32[4,3,1024]{2,1,0:T(4,128)} %copy.12.conv_ref, bf16[2304,128]{1,0:T(8,128)(2,1)} %down_hbm.1, ...), custom_call_target="tpu_custom_call" | custom-call | tf_op jit(solution)/shard_map/local/pallas_call | solution.py:428
  94.7 2.3 %copy.16 = bf16[512,1024]{1,0:T(8,128)(2,1)} copy(bf16[512,1024]{1,0:T(8,128)(2,1)} %get-tuple-element.4) | data formatting | bytes 2097152
  96.9 2.3 %copy.17 = f32[2,8,128,128]{3,2,1,0:T(8,128)} copy(f32[2,8,128,128]{3,2,1,0:T(8,128)} %get-tuple-element.5) | data formatting | bytes 2097152

commit v4 on v3

--- a/solution.py
+++ b/solution.py
@@ -21,6 +21,22 @@
     if dims is None:
         return jnp.dot(left, right, preferred_element_type=F32)
     return lax.dot_general(left, right, dims, preferred_element_type=F32)
+
+
+def diagonal(one, two):
+    top = jnp.concatenate([one, jnp.zeros(one.shape[:1] + two.shape[1:], BF16)], axis=1)
+    low = jnp.concatenate([jnp.zeros(two.shape[:1] + one.shape[1:], BF16), two], axis=1)
+    return jnp.concatenate([top, low], axis=0)
+
+
+def twin_dots(left, right, dims=None):
+    out = []
+    for h in range(0, len(left), 2):
+        wide = jnp.concatenate([left[h].astype(BF16), left[h + 1].astype(BF16)], axis=1)
+        both = dot(wide, diagonal(right[h].astype(BF16), right[h + 1].astype(BF16)), dims)
+        middle = both.shape[1] // 2
+        out += [both[:, :middle], both[:, middle:]]
+    return out
 
 
 def softplus(value):
@@ -74,9 +90,10 @@
     dim = gu_ref.shape[1] // num_heads
     group = min(4, num_heads)
     span = group * dim
-    taps = conv_ref.shape[0]
+    taps = conv_ref.shape[1]
     ctx, place = lax.axis_index("ctx"), lax.axis_index("head")
     rank = ctx * num_blocks + place
+    position = pos_ref[ctx // 2] - ctx * (num_blocks * chunk)
     ranks = num_ctx * num_blocks
     after, before = (rank + 1) % ranks, (rank + ranks - 1) % ranks
     next_id = {"ctx": after // num_blocks, "head": after % num_blocks}
@@ -164,9 +181,9 @@
         rows = pl.ds(first_row, chunk)
         own_rows = buf[block, HALO:, :]
         latent_ref[...] = jnp.dot(own_rows, down_ref[...], preferred_element_type=F32).astype(BF16)
-        beta_ref[...] = jnp.dot(own_rows, wb_ref[...], preferred_element_type=F32)
+        beta_ref[...] = dot(own_rows, wb_ref[...], NT)
         halo_keep = jnp.where(ctx * num_blocks + block == 0, 0.0, 1.0).astype(F32)
-        inner = pos_ref[0] - block * chunk
+        inner = position - block * chunk
         here = (inner >= 0) & (inner < chunk)
 
         def head_group(hg, carry):
@@ -179,7 +196,7 @@
                 ext_ref[j, HALO:, :] = proj[HALO:]
                 start = HALO + 1 - taps
                 mixed = sum(
-                    conv_ref[tap, j : j + 1, cols] * ext_ref[j, start + tap : start + tap + chunk, :]
+                    conv_ref[j, tap : tap + 1, cols] * ext_ref[j, start + tap : start + tap + chunk, :]
                     for tap in range(taps)
                 )
                 acts.append(mixed / (1.0 + jnp.exp(-mixed)))
@@ -213,17 +230,16 @@
                 scale = jnp.exp(-jnp.abs(cum - level_reference(cum, size)))
                 ks = (key * scale).astype(BF16)
                 qs = (query * scale).astype(BF16)
-                pairs = [
-                    dot(jnp.concatenate([cut(ks, h), cut(qs, h)], axis=0), cut(ks, h), NT) for h in heads
-                ]
+                both = jnp.concatenate([ks, qs], axis=0)
+                pairs = twin_dots([cut(both, h) for h in heads], [cut(ks, h) for h in heads], NT)
                 pair_k = [jnp.where(mask, p[:chunk], old) for p, old in zip(pairs, pair_k)]
                 pair_q = [jnp.where(mask, p[chunk:], old) for p, old in zip(pairs, pair_q)]
             system = [betas[h] * pair_k[h] for h in heads]
             inverse = [eye - jnp.where(masks[1], system[h], 0.0) for h in heads]
             for size, mask in masks.items():
                 if size > 1:
-                    left = [dot(inverse[h], jnp.where(mask, system[h], 0.0)) for h in heads]
-                    right = [dot(left[h], inverse[h]) for h in heads]
+                    left = twin_dots(inverse, [jnp.where(mask, system[h], 0.0) for h in heads])
+                    right = twin_dots(left, inverse)
                     inverse = [inverse[h] - right[h] for h in heads]
             grown = jnp.exp(cum)
             key_up = key * grown
@@ -315,8 +331,8 @@
         lax.fori_loop(0, groups, one, 0)
 
     pair = 2
-    which = pos_ref[1]
-    owned = (pos_ref[0] >= 0) & (pos_ref[0] < num_blocks * chunk)
+    which = jnp.clip(position, 0, num_blocks * chunk - 1) // chunk
+    owned = (position >= 0) & (position < num_blocks * chunk)
 
     def read(j, carry):
         @pl.when(ctx == j)
@@ -382,7 +398,7 @@
         share(turn, (ctx + turn) % num_ctx).wait_recv()
     for turn in range(1, num_ctx):
         share(turn, ctx).wait_send()
-    forks_ref[...] = fork_ref[...].astype(F32)
+    forks_ref[...] = fork_ref[...]
 
     @pl.when(ctx < num_ctx - 1)
     def _():
@@ -414,10 +430,7 @@
     num_ctx = lax.axis_size("ctx")
     num_forks = fork_pos.shape[0]
     per_fork = num_ctx // num_forks
-    ctx = lax.axis_index("ctx")
     assert per_fork == 2 and num_heads % 2 == 0
-    pos = lax.dynamic_slice(fork_pos, (ctx // per_fork,), (1,)) - ctx * seq_len
-    pos = jnp.concatenate([pos, jnp.clip(pos, 0, seq_len - 1) // chunk])
     span = min(4, num_heads) * dim
 
     smem = pl.BlockSpec(memory_space=pltpu.SMEM)
@@ -425,13 +438,13 @@
     hbm = pl.BlockSpec(memory_space=pl.ANY)
     cols = lambda dtype: pltpu.VMEM((seq_len, head_cols), dtype)
     heads = lambda dtype, *shape: pltpu.VMEM((num_heads,) + shape, dtype)
-    return pl.pallas_call(
+    attended, forks = pl.pallas_call(
         functools.partial(local_kernel, num_ctx, num_blocks),
         in_specs=[vmem, hbm, hbm, hbm, vmem, hbm, vmem, vmem, smem, smem],
         out_specs=[vmem] * 2,
         out_shape=[
             jax.ShapeDtypeStruct((seq_len, head_cols), BF16),
-            jax.ShapeDtypeStruct((num_forks, num_heads, dim, dim), F32),
+            jax.ShapeDtypeStruct((num_forks, num_heads, dim, dim), BF16),
         ],
         scratch_shapes=[
             cols(BF16), cols(F32), heads(BF16, seq_len, chunk), cols(BF16), cols(BF16),
@@ -466,7 +479,8 @@
             collective_id=0, has_side_effects=True, vmem_limit_bytes=60 << 20
         ),
         name="local",
-    )(activations, w_query, w_key, w_value, conv_weight, gate_down, gate_up, w_beta, decay_rate, pos)
+    )(activations, w_query, w_key, w_value, conv_weight.transpose(1, 0, 2), gate_down, gate_up, w_beta.T, decay_rate, fork_pos)
+    return attended, forks.astype(F32)
 
 
 def solution(mesh):

time: 101 us -> 94.5 us (0.936)
  local copies, waits for them, and re-layouts: 9.09 us -> 2.26 us
  other arithmetic: 0.62 us -> 2.12 us
    unnamed x4 -> x1, local copies, waits for them, and re-layouts: 7.84 us -> 2.26 us
    convert_element_type x0 -> x1, other arithmetic: none -> 2.12 us  [per_device(): return (attended, forks.astype(F32))]
    dynamic_slice x1 -> x0, local copies, waits for them, and re-layouts: 1.24 us -> none  [per_device(): pos = lax.dynamic_slice(fork_pos, (ctx // per_fork,), (1,)) - ctx * seq_len]
where the time goes in v4:
time: 94.5 us; the launch traced here: 92.7 us
  Pallas kernels  87.7 us (93%)
  local copies, waits for them, and re-layouts  2.26 us (2%)
  other arithmetic  2.12 us (2%)
    pallas_call x1, Pallas kernels, per_device(): pl.pallas_call(functools.partial(local_kernel, num_ctx, num_blocks), in_s...  87.7 us
    unnamed x1, local copies, waits for them, and re-layouts  2.26 us
    convert_element_type x1, other arithmetic, per_device(): return (attended, forks.astype(F32))  2.12 us

profile of v4, /device:TPU:0, one launch (start us, length us, event | category | flops | bytes accessed | tf_op | source)
XLA Modules:
  0.0 92.7 jit_solution(1621057278724189690)
XLA Ops:
  0.6 87.7 %local.1 = (bf16[512,1024]{1,0:T(8,128)(2,1)}, bf16[2,8,128,128]{3,2,1,0:T(8,128)(2,1)}) custom-call(bf16[128,2304]{1,0:T(8,128)(2,1)} %act_ref.1, bf16[2304,1024]{1,0:T(8,128)(2,1)} %wq_hbm.1, bf16[2304,1024]{1,0:T(8,128)(2,1)} %wk_hbm.1, bf16[2304,1024]{1,0:T(8,128)(2,1)} %wv_hbm.1, f32[3,4,1024]{2,1,0:T(4,128)} %bitcast.2, bf16[2304,128]{1,0:T(8,128)(2,1)} %down_hbm.1, ...), custom_call_target="tpu_custom_call" | custom-call | tf_op jit(solution)/shard_map/local/pallas_call | solution.py:441
  88.3 2.1 %convert_element_type.3 = f32[2,8,128,128]{3,2,1,0:T(8,128)} convert(bf16[2,8,128,128]{3,2,1,0:T(8,128)(2,1)} %get-tuple-element.5) | non-fusion elementwise | flops 262144 | bytes 1572864 | tf_op jit(solution)/shard_map/convert_element_type | solution.py:483
  90.4 2.3 %copy.13 = bf16[512,1024]{1,0:T(8,128)(2,1)} copy(bf16[512,1024]{1,0:T(8,128)(2,1)} %get-tuple-element.8) | data formatting | bytes 2097152

commit v5 on v4

--- a/solution.py
+++ b/solution.py
@@ -8,7 +8,7 @@
 from jax.experimental.pallas import tpu as pltpu
 from jax.sharding import PartitionSpec as P
 
-HALO = 16
+HALO = 8
 MESH = pl.DeviceIdType.MESH
 F32 = jnp.float32
 BF16 = jnp.bfloat16

time: 94.5 us -> 91.5 us (0.968)
  Pallas kernels: 87.7 us -> 84.7 us
    pallas_call x1, Pallas kernels: 87.7 us -> 84.7 us  [per_device(): pl.pallas_call(functools.partial(local_kernel, num_ctx, num_blocks), in_s...]
where the time goes in v5:
time: 91.5 us; the launch traced here: 89.7 us
  Pallas kernels  84.7 us (93%)
  local copies, waits for them, and re-layouts  2.26 us (2%)
  other arithmetic  2.12 us (2%)
    pallas_call x1, Pallas kernels, per_device(): pl.pallas_call(functools.partial(local_kernel, num_ctx, num_blocks), in_s...  84.7 us
    unnamed x1, local copies, waits for them, and re-layouts  2.26 us
    convert_element_type x1, other arithmetic, per_device(): return (attended, forks.astype(F32))  2.12 us

profile of v5, /device:TPU:0, one launch (start us, length us, event | category | flops | bytes accessed | tf_op | source)
XLA Modules:
  0.0 89.7 jit_solution(16272483060199775332)
XLA Ops:
  0.6 84.7 %local.1 = (bf16[512,1024]{1,0:T(8,128)(2,1)}, bf16[2,8,128,128]{3,2,1,0:T(8,128)(2,1)}) custom-call(bf16[128,2304]{1,0:T(8,128)(2,1)} %act_ref.1, bf16[2304,1024]{1,0:T(8,128)(2,1)} %wq_hbm.1, bf16[2304,1024]{1,0:T(8,128)(2,1)} %wk_hbm.1, bf16[2304,1024]{1,0:T(8,128)(2,1)} %wv_hbm.1, f32[3,4,1024]{2,1,0:T(4,128)} %bitcast.2, bf16[2304,128]{1,0:T(8,128)(2,1)} %down_hbm.1, ...), custom_call_target="tpu_custom_call" | custom-call | tf_op jit(solution)/shard_map/local/pallas_call | solution.py:441
  85.3 2.1 %convert_element_type.3 = f32[2,8,128,128]{3,2,1,0:T(8,128)} convert(bf16[2,8,128,128]{3,2,1,0:T(8,128)(2,1)} %get-tuple-element.5) | non-fusion elementwise | flops 262144 | bytes 1572864 | tf_op jit(solution)/shard_map/convert_element_type | solution.py:483
  87.4 2.3 %copy.13 = bf16[512,1024]{1,0:T(8,128)(2,1)} copy(bf16[512,1024]{1,0:T(8,128)(2,1)} %get-tuple-element.8) | data formatting | bytes 2097152
